TPU v7x, 256 devices: a whole 4x4x8 slice. The times are simulated.
256 devices in a mesh: inline: 32 (over x, y, core), xline: 8 (over z).
Axes of the slice: x: 4, y: 4, z: 8, core: 2. Of those that a mesh axis runs over, the one named last changes fastest.
Arguments:
- traces: bfloat16 [65536, 2048], P(('inline', 'xline')), may hold values from -6 to 6
- owners: int32 [65536, 1], P(('inline', 'xline')), may hold values from 0 to 255, as said below
- midpoint: int32 [65536], P(('inline', 'xline')), may hold values from 0 to 7
- offset_class: int32 [65536], P(('inline', 'xline')), may hold values from 0 to 3
- offsets: float32 [4], replicated, may hold values from 51 to 1024
- velocities: float32 [16], replicated, may hold values from 1 to 4
Outputs:
- stacked: bfloat16 [2048, 16, 2048], P(('inline', 'xline'))
- semblance: float32 [2048, 16, 2048], P(('inline', 'xline'))
Inputs may be any that keep to these rules, and one draw needn't show every extreme that they name: The 256 traces of one device name one owner at most 2 times; some owners receive 2 traces from every device, and some owners receive none.
All inputs are finite; a program needn't handle non-finite values.
Results may differ from a plain program's by a relative error of at most 0.0053.
Values may be sent and summed in bfloat16 or wider, within the bound.
A program may use at most 64 MiB of HBM per device.

v0:
```python
import math

import jax
import jax.numpy as jnp
from jax import lax
from jax.sharding import PartitionSpec as P

HALF_WIN = 4
CMP_DEV = 8


def with_halo(block, sides, width):
    for axis, dim in sides:
        count = lax.axis_size(axis)
        forward = [(i, i + 1) for i in range(count - 1)]
        backward = [(target, source) for source, target in forward]
        low = lax.ppermute(
            lax.slice_in_dim(block, block.shape[dim] - width, None, axis=dim), axis, forward
        )
        high = lax.ppermute(lax.slice_in_dim(block, 0, width, axis=dim), axis, backward)
        block = jnp.concatenate([low, block, high], axis=dim)
    return block


def window_sum(values):
    length = values.shape[-1]
    padded = jnp.pad(values, [(0, 0)] * (values.ndim - 1) + [(HALF_WIN, HALF_WIN)])
    summed = padded[..., 0:length]
    for offset in range(1, 2 * HALF_WIN + 1):
        summed = summed + padded[..., offset : offset + length]
    return summed


def panels(binned, offsets, velocities):
    classes, midpoints, samples = binned.shape
    block_len = math.gcd(128, samples)
    window_len = block_len + 8
    block_count = samples // block_len
    padded = jnp.pad(binned, ((0, 0), (0, 0), (0, window_len)))
    sample_time = jnp.arange(samples).astype(jnp.float32)
    row_grid = jnp.arange(window_len)[:, None]

    def cut_window(plane_rows, start_at):
        return lax.dynamic_slice_in_dim(plane_rows, start_at, window_len, 1)

    cut_blocks = jax.vmap(cut_window, (None, 0))
    cut_classes = jax.vmap(cut_blocks, (0, 0))
    cut_velocities = jax.vmap(cut_classes, (None, 0))

    def per_group(velocity_group):
        vel_count = velocity_group.shape[0]
        slowness = offsets[None, :] / velocity_group[:, None]
        position = jnp.sqrt(
            sample_time[None, None, :] * sample_time[None, None, :]
            + (slowness * slowness)[:, :, None]
        )
        floored = jnp.floor(position)
        fraction = position - floored
        sample_index = jnp.minimum(floored, float(samples)).astype(jnp.int32)
        sample_index = sample_index.reshape(vel_count, classes, block_count, block_len)
        begins = sample_index[..., 0]
        local_row = (sample_index - begins[..., None])[..., None, :]
        low_weight = (
            (1.0 - fraction)
            .astype(jnp.bfloat16)
            .reshape(vel_count, classes, block_count, 1, block_len)
        )
        high_weight = fraction.astype(jnp.bfloat16).reshape(
            vel_count, classes, block_count, 1, block_len
        )
        weights = jnp.where(
            row_grid == local_row,
            low_weight,
            jnp.where(row_grid == local_row + 1, high_weight, jnp.zeros((), jnp.bfloat16)),
        )
        windows = cut_velocities(padded, begins)
        moved_out = jnp.einsum(
            "ghbmr,ghbrq->gmhbq", windows, weights, preferred_element_type=jnp.float32
        )
        summed = jnp.sum(moved_out, axis=2).reshape(vel_count, midpoints, samples)
        energy = jnp.sum(moved_out * moved_out, axis=2).reshape(vel_count, midpoints, samples)
        return (summed, energy)

    vel_group = math.gcd(4, velocities.shape[0])
    summed, energy = lax.map(per_group, velocities.reshape(-1, vel_group))
    summed = jnp.transpose(summed, (2, 0, 1, 3)).reshape(midpoints, -1, samples)
    energy = jnp.transpose(energy, (2, 0, 1, 3)).reshape(midpoints, -1, samples)
    return (summed, energy)


def per_device(traces, owners, midpoint, offset_class, offsets, velocities):
    inline_count = lax.axis_size("inline")
    xline_count = lax.axis_size("xline")
    devices = inline_count * xline_count
    trace_rows, samples = traces.shape
    classes = offsets.shape[0]
    capacity = max(2, 2 * trace_rows // devices)
    target = owners[:, 0]
    onehot_dest = (target[:, None] == jnp.arange(devices)[None, :]).astype(jnp.int32)
    slot_rank = jnp.sum((jnp.cumsum(onehot_dest, axis=0) - onehot_dest) * onehot_dest, axis=1)
    slot_row = target * capacity + slot_rank
    buffer = jnp.zeros((devices * capacity, samples), traces.dtype).at[slot_row].set(traces)
    slot_keys = (
        jnp.full((devices * capacity,), -1, jnp.int32)
        .at[slot_row]
        .set(offset_class * CMP_DEV + midpoint)
    )
    buffer = buffer.reshape(inline_count, xline_count, capacity, samples)
    slot_keys = slot_keys.reshape(inline_count, xline_count, capacity)
    arrived, arrived_keys = (
        lax.all_to_all(
            lax.all_to_all(buffer, "inline", split_axis=0, concat_axis=0, tiled=True),
            "xline",
            split_axis=1,
            concat_axis=1,
            tiled=True,
        ),
        lax.all_to_all(
            lax.all_to_all(slot_keys, "inline", split_axis=0, concat_axis=0, tiled=True),
            "xline",
            split_axis=1,
            concat_axis=1,
            tiled=True,
        ),
    )
    arrived = arrived.reshape(-1, samples)
    arrived_keys = arrived_keys.reshape(-1)
    members = arrived_keys[None, :] == jnp.arange(classes * CMP_DEV)[:, None]
    gathers = jnp.dot(members.astype(jnp.bfloat16), arrived, preferred_element_type=jnp.float32)
    binned = gathers.astype(jnp.bfloat16).reshape(classes, CMP_DEV, samples)
    global_mid = target * CMP_DEV + midpoint
    histogram = jax.ops.segment_sum(
        jnp.ones((trace_rows,), jnp.float32), global_mid, devices * CMP_DEV
    )
    fold_count = lax.psum_scatter(histogram, ("inline", "xline"), scatter_dimension=0, tiled=True)
    summed, energy = panels(binned, offsets, velocities)
    planes = jnp.stack([window_sum(summed * summed), window_sum(energy)])
    rimmed = with_halo(planes, ((("inline", "xline"), 1),), 1)
    smoothed = rimmed[:, 0:-2] + rimmed[:, 1:-1] + rimmed[:, 2:]
    numerator = smoothed[0]
    denominator = smoothed[1]
    stacked = (summed / jnp.maximum(fold_count, 1.0)[:, None, None]).astype(jnp.bfloat16)
    semblance = numerator / jnp.maximum(classes * denominator, 1.0)
    return (stacked, semblance)


def solution(mesh):
    in_specs = (
        P(("inline", "xline"), None),
        P(("inline", "xline"), None),
        P(("inline", "xline")),
        P(("inline", "xline")),
        P(),
        P(),
    )
    out_specs = (P(("inline", "xline"), None, None), P(("inline", "xline"), None, None))
    return jax.shard_map(
        per_device, mesh=mesh, in_specs=in_specs, out_specs=out_specs, check_vma=False
    )
```

profile of v0, /device:TPU:1, one launch (start us, length us, event | category | flops | bytes accessed | tf_op | source)
XLA Modules:
  0.0 435.3 jit_solution(4086104306672651795)
XLA Ops:
  6.4 8.6 %all-to-all-start = ((s32[32,8,2]{1,2,0:T(2,128)}), s32[32,8,2]{1,2,0:T(2,128)S(1)}, u32[]{:S(2)}, u32[]{:S(2)}) async-start(s32[32,8,2]{1,2,0:T(2,128)} %copy.84), calls=%async_computation | async-start | bytes 65536 | tf_op jit(solution)/shard_map/all_to_all | solution.py:119
  15.0 3.5 scatter_custom_fusion.1
  22.3 6.3 %all-to-all-start.2 = ((bf16[32,8,2,2048]{3,2,1,0:T(2,128)(2,1)}), bf16[32,8,2,2048]{3,2,1,0:T(2,128)(2,1)S(1)}, u32[]{:S(2)}, u32[]{:S(2)}) async-start(bf16[32,8,2,2048]{3,2,1,0:T(2,128)(2,1)} %reshape.132), calls=%async_computation.2 | async-start | bytes 4194304 | tf_op jit(solution)/shard_map/all_to_all | solution.py:112
  29.3 27.7 %all-to-all-done.2 = bf16[32,8,2,2048]{3,2,1,0:T(2,128)(2,1)S(1)} async-done(((bf16[32,8,2,2048]{3,2,1,0:T(2,128)(2,1)}), bf16[32,8,2,2048]{3,2,1,0:T(2,128)(2,1)S(1)}, u32[]{:S(2)}, u32[]{:S(2)}) %all-to-all-start.2) | async-done | bytes 2097184 | tf_op jit(solution)/shard_map/all_to_all | solution.py:112
  56.9 8.2 %all-to-all-start.1 = ((s32[32,8,2]{0,2,1:T(2,128)}), s32[32,8,2]{0,2,1:T(2,128)S(1)}, u32[]{:S(2)}, u32[]{:S(2)}) async-start(s32[32,8,2]{0,2,1:T(2,128)} %copy.85), calls=%async_computation.1 | async-start | bytes 16384 | tf_op jit(solution)/shard_map/all_to_all | solution.py:118
  65.1 3.1 copy.87
  68.3 3.4 all-to-all-done.1
  71.7 3.6 all-to-all-start.3
  77.4 88.8 %all-reduce.4 = f32[2048]{0:T(1024)S(1)} all-reduce(f32[2048]{0:T(1024)S(1)} %scatter_custom_fusion.2), channel_id=2, replica_groups=mesh['inline'=32,'xline'=8] {'inline','xline'}, use_global_device_ids=true, to_apply=%region_10.11.clone | all-reduce | flops 2048 | bytes 16384
  166.5 3.6 copy.88
  175.8 3.1 pad.14
  179.0 234.6 %while.16 = (s32[]{:T(128)}, f32[4,4,8,2048]{3,2,1,0:T(8,128)}, f32[4,4,8,2048]{3,2,1,0:T(8,128)}, f32[4]{0:T(128)S(1)}, f32[4,4]{1,0:T(4,128)S(1)}, /*index=5*/bf16[4,8,2184]{1,0,2:T(4,128)(2,1)S(1)}, s32[]{:T(128)}) while((s32[]{:T(128)}, f32[4,4,8,2048]{3,2,1,0:T(8,128)}, f32[4,4,8,2048]{3,2,1,0:T(8,128)}, ...), condition=%wide.region_8.9_spmd.clone.clone, body=%wide.region_5.0_spmd.clone.clone.sunk | while | flops 90249248 | bytes 4195677 | solution.py:85
  196.3 42.2 %gather_fusion = bf16[256,8,136]{1,0,2:T(8,128)(2,1)} fusion(bf16[4,8,2184]{1,0,2:T(4,128)(2,1)S(1)} %get-tuple-element.246, s32[256]{0:T(256)S(1)} %reshape.185), kind=kCustom, calls=%fused_computation.clone.clone.1 | custom fusion | bytes 1117184 | tf_op jit(solution)/shard_map/while/body/eval_jaxpr/vmap(vmap(vmap()))/gather | solution.py:44
  238.5 10.0 %multiply_reduce_fusion.2 = (f32[4,8,16,128]{3,1,2,0:T(8,128)S(1)}, f32[4,8,16,128]{3,1,2,0:T(8,128)S(1)}) fusion(bf16[4,4,16,8,136]{3,2,1,0,4:T(8,128)(2,1)} %bitcast.52, s32[4,4,16,128]{3,2,1,0:T(8,128)S(1)} %get-tuple-element.219, s32[4,4,16,128]{3,2,1,0:T(8,128)S(1)} %get-tuple-element.220, bf16[4,4,16,128]{3,2,1,0:T(8,128)(2,1)S(1)} %get-tuple-element.221, ...), kind=kOutput, calls=%fused_computation.18.clone.1 | convolution fusion | flops 89784320 | bytes 1474560 | tf_op jit(solution)/shard_map/while/body/eval_jaxpr/ghbmr,ghbrq->gmhbq/dot_general | solution.py:77
  250.4 43.2 %gather_fusion = bf16[256,8,136]{1,0,2:T(8,128)(2,1)} fusion(bf16[4,8,2184]{1,0,2:T(4,128)(2,1)S(1)} %get-tuple-element.246, s32[256]{0:T(256)S(1)} %reshape.185), kind=kCustom, calls=%fused_computation.clone.clone.1 | custom fusion | bytes 1117184 | tf_op jit(solution)/shard_map/while/body/eval_jaxpr/vmap(vmap(vmap()))/gather | solution.py:44
  293.6 10.0 %multiply_reduce_fusion.2 = (f32[4,8,16,128]{3,1,2,0:T(8,128)S(1)}, f32[4,8,16,128]{3,1,2,0:T(8,128)S(1)}) fusion(bf16[4,4,16,8,136]{3,2,1,0,4:T(8,128)(2,1)} %bitcast.52, s32[4,4,16,128]{3,2,1,0:T(8,128)S(1)} %get-tuple-element.219, s32[4,4,16,128]{3,2,1,0:T(8,128)S(1)} %get-tuple-element.220, bf16[4,4,16,128]{3,2,1,0:T(8,128)(2,1)S(1)} %get-tuple-element.221, ...), kind=kOutput, calls=%fused_computation.18.clone.1 | convolution fusion | flops 89784320 | bytes 1474560 | tf_op jit(solution)/shard_map/while/body/eval_jaxpr/ghbmr,ghbrq->gmhbq/dot_general | solution.py:77
  305.5 42.3 %gather_fusion = bf16[256,8,136]{1,0,2:T(8,128)(2,1)} fusion(bf16[4,8,2184]{1,0,2:T(4,128)(2,1)S(1)} %get-tuple-element.246, s32[256]{0:T(256)S(1)} %reshape.185), kind=kCustom, calls=%fused_computation.clone.clone.1 | custom fusion | bytes 1117184 | tf_op jit(solution)/shard_map/while/body/eval_jaxpr/vmap(vmap(vmap()))/gather | solution.py:44
  347.8 10.0 %multiply_reduce_fusion.2 = (f32[4,8,16,128]{3,1,2,0:T(8,128)S(1)}, f32[4,8,16,128]{3,1,2,0:T(8,128)S(1)}) fusion(bf16[4,4,16,8,136]{3,2,1,0,4:T(8,128)(2,1)} %bitcast.52, s32[4,4,16,128]{3,2,1,0:T(8,128)S(1)} %get-tuple-element.219, s32[4,4,16,128]{3,2,1,0:T(8,128)S(1)} %get-tuple-element.220, bf16[4,4,16,128]{3,2,1,0:T(8,128)(2,1)S(1)} %get-tuple-element.221, ...), kind=kOutput, calls=%fused_computation.18.clone.1 | convolution fusion | flops 89784320 | bytes 1474560 | tf_op jit(solution)/shard_map/while/body/eval_jaxpr/ghbmr,ghbrq->gmhbq/dot_general | solution.py:77
  359.8 42.8 %gather_fusion = bf16[256,8,136]{1,0,2:T(8,128)(2,1)} fusion(bf16[4,8,2184]{1,0,2:T(4,128)(2,1)S(1)} %get-tuple-element.246, s32[256]{0:T(256)S(1)} %reshape.185), kind=kCustom, calls=%fused_computation.clone.clone.1 | custom fusion | bytes 1117184 | tf_op jit(solution)/shard_map/while/body/eval_jaxpr/vmap(vmap(vmap()))/gather | solution.py:44
  402.5 10.0 %multiply_reduce_fusion.2 = (f32[4,8,16,128]{3,1,2,0:T(8,128)S(1)}, f32[4,8,16,128]{3,1,2,0:T(8,128)S(1)}) fusion(bf16[4,4,16,8,136]{3,2,1,0,4:T(8,128)(2,1)} %bitcast.52, s32[4,4,16,128]{3,2,1,0:T(8,128)S(1)} %get-tuple-element.219, s32[4,4,16,128]{3,2,1,0:T(8,128)S(1)} %get-tuple-element.220, bf16[4,4,16,128]{3,2,1,0:T(8,128)(2,1)S(1)} %get-tuple-element.221, ...), kind=kOutput, calls=%fused_computation.18.clone.1 | convolution fusion | flops 89784320 | bytes 1474560 | tf_op jit(solution)/shard_map/while/body/eval_jaxpr/ghbmr,ghbrq->gmhbq/dot_general | solution.py:77
  416.9 4.5 %add_bitcast_fusion = (f32[1,8,16,2048]{3,2,1,0:T(8,128)S(1)}, f32[1,8,16,2048]{3,2,1,0:T(8,128)S(1)}) fusion(f32[8,16,2048]{2,1,0:T(8,128)S(1)} %copy.93, f32[8,16,2048]{2,1,0:T(8,128)S(1)} %get-tuple-element.162), kind=kLoop, calls=%fused_computation.57 | loop fusion | flops 4194304 | bytes 4194304 | tf_op jit(solution)/shard_map/stack | solution.py:137
  421.4 3.4 collective-permute-start
  424.8 3.5 collective-permute-start.1
  428.3 4.7 %collective-permute-done = f32[2,1,16,2048]{3,2,1,0:T(8,128)S(1)} collective-permute-done((f32[2,1,16,2048]{3,2,1,0:T(8,128)S(1)}, f32[2,1,16,2048]{3,2,1,0:T(8,128)S(1)}, u32[]{:S(2)}, u32[]{:S(2)}) %collective-permute-start) | collective-permute-done | bytes 262176 | tf_op jit(solution)/shard_map/ppermute | solution.py:17
  (73 shorter events, 31.3 us)
Async XLA Ops:
  6.4 15.9 %all-to-all-start = ((s32[32,8,2]{1,2,0:T(2,128)}), s32[32,8,2]{1,2,0:T(2,128)S(1)}, u32[]{:S(2)}, u32[]{:S(2)}) async-start(s32[32,8,2]{1,2,0:T(2,128)} %copy.84), calls=%async_computation | async-start | bytes 65536 | tf_op jit(solution)/shard_map/all_to_all | solution.py:119
  22.3 34.6 %all-to-all-start.2 = ((bf16[32,8,2,2048]{3,2,1,0:T(2,128)(2,1)}), bf16[32,8,2,2048]{3,2,1,0:T(2,128)(2,1)S(1)}, u32[]{:S(2)}, u32[]{:S(2)}) async-start(bf16[32,8,2,2048]{3,2,1,0:T(2,128)(2,1)} %reshape.132), calls=%async_computation.2 | async-start | bytes 4194304 | tf_op jit(solution)/shard_map/all_to_all | solution.py:112
  56.9 14.8 %all-to-all-start.1 = ((s32[32,8,2]{0,2,1:T(2,128)}), s32[32,8,2]{0,2,1:T(2,128)S(1)}, u32[]{:S(2)}, u32[]{:S(2)}) async-start(s32[32,8,2]{0,2,1:T(2,128)} %copy.85), calls=%async_computation.1 | async-start | bytes 16384 | tf_op jit(solution)/shard_map/all_to_all | solution.py:118
  68.3 7.1 %copy-start.2 = (f32[16]{0:T(128)S(1)}, f32[16]{0:T(128)}, u32[]{:S(2)}) copy-start(f32[16]{0:T(128)} %param.13) | copy-start | bytes 196
  71.7 94.8 %all-to-all-start.3 = ((bf16[32,8,2,2048]{3,2,0,1:T(2,128)(2,1)}), bf16[32,8,2,2048]{3,2,0,1:T(2,128)(2,1)S(1)}, u32[]{:S(2)}, u32[]{:S(2)}) async-start(bf16[32,8,2,2048]{3,2,0,1:T(2,128)(2,1)} %copy.87), calls=%async_computation.3 | async-start | bytes 4194304 | tf_op jit(solution)/shard_map/all_to_all | solution.py:111
  175.8 3.1 copy-start.1
  413.5 1.9 copy-start
  421.4 11.5 %collective-permute-start = (f32[2,1,16,2048]{3,2,1,0:T(8,128)S(1)}, f32[2,1,16,2048]{3,2,1,0:T(8,128)S(1)}, u32[]{:S(2)}, u32[]{:S(2)}) collective-permute-start(f32[2,1,16,2048]{3,2,1,0:T(8,128)S(1)} %get-tuple-element.160), channel_id=1, source_target_pairs={{0,1},{1,2},{2,3},{3,4},{4,5},{5,6},{6,7},{7,8},{8,9},{9,10},{10,1... | collective-permute-start | bytes 786440 | tf_op jit(solution)/shard_map/ppermute | solution.py:17
  424.8 8.8 %collective-permute-start.1 = (f32[2,1,16,2048]{3,2,1,0:T(8,128)S(1)}, f32[2,1,16,2048]{3,2,1,0:T(8,128)S(1)}, u32[]{:S(2)}, u32[]{:S(2)}) collective-permute-start(f32[2,1,16,2048]{3,2,1,0:T(8,128)S(1)} %get-tuple-element.161), channel_id=1, source_target_pairs={{1,0},{2,1},{3,2},{4,3},{5,4},{6,5},{7,6},{8,7},{9,8},{10,9},{11,1... | collective-permute-start | bytes 786440 | tf_op jit(solution)/shard_map/ppermute | solution.py:20
where the time goes:
time: 444 us; the launch traced here: 435 us
  local copies, waits for them, and re-layouts  202 us (45%)
  blocking collectives  88.8 us (20%)
  matrix products  40.4 us (9%)
  waiting for transfers between devices  37.5 us (8%)
  starting transfers between devices  33.5 us (8%)
  loops' own time  16.5 us (4%)
  other arithmetic  15.8 us (4%)
    gather x8, local copies, waits for them, and re-layouts, cut_window(): return lax.dynamic_slice_in_dim(plane_rows, start_at, window_len, 1)  171 us
    unnamed x1, blocking collectives  88.8 us
    dot_general x4, matrix products, per_group(): jnp.einsum('ghbmr,ghbrq->gmhbq', windows, weights, preferred_element_type...  39.9 us
    all_to_all x1, waiting for transfers between devices, per_device(): lax.all_to_all(buffer, 'inline', split_axis=0, concat_axis=0, tiled=True)  27.7 us
    another operation x1, loops' own time, panels(): summed, energy = lax.map(per_group, velocities.reshape(-1, vel_group))  16.5 us
  transfers between devices with their start and end apart: 6, of which 5 were waited for; matrix products, arithmetic and copies ran while one was open for 3% of the time, Pallas kernels for 0%

commit v1 on v0

v1 whole, which is shorter than its diff:
```python
import functools

import jax
import jax.numpy as jnp
from jax import lax
from jax.experimental import pallas as pl
from jax.experimental.pallas import tpu as pltpu
from jax.sharding import PartitionSpec as P

CMP_DEV = 8

LANES = 128
GROUP = 8


def take_lanes(values, index):
    return jnp.take_along_axis(values, index, axis=1, mode="promise_in_bounds")


def panels_kernel(
    start_ref, slow_ref, x_ref, fold_ref, stacked_ref, semblance_ref,
    low_at, high_at, low_w, high_w, power, energy, sums, ratio,
):
    vels, mids, samples = semblance_ref.shape[1], semblance_ref.shape[0], semblance_ref.shape[2]
    classes = x_ref.shape[0]
    blocks = samples // LANES

    def prepare(gh, _):
        row = lax.broadcasted_iota(jnp.int32, (blocks, LANES), 0)
        lane = lax.broadcasted_iota(jnp.int32, (blocks, LANES), 1)
        time = (row * LANES + lane).astype(jnp.float32)
        position = jnp.sqrt(time * time + slow_ref[gh])
        floored = jnp.floor(position)
        fraction = position - floored
        index = jnp.minimum(floored, float(samples)).astype(jnp.int32)
        rows = pl.ds(pl.multiple_of(gh * blocks, blocks), blocks)
        low_at[rows, :] = index & (LANES - 1)
        high_at[rows, :] = (index + 1) & (LANES - 1)
        low_w[rows, :] = (1.0 - fraction).astype(jnp.bfloat16).astype(jnp.float32)
        high_w[rows, :] = fraction.astype(jnp.bfloat16).astype(jnp.float32)
        return 0

    lax.fori_loop(0, vels * classes, prepare, 0)

    edge = jnp.zeros((mids, LANES), jnp.float32)
    for g in range(vels):
        for plane in (power, energy):
            plane[g * mids:(g + 1) * mids, 0:LANES] = edge
            plane[g * mids:(g + 1) * mids, LANES + samples:] = edge

    shape = (mids, LANES)
    lane = lax.broadcasted_iota(jnp.int32, shape, 1)
    sub = lax.broadcasted_iota(jnp.int32, shape, 0)
    scale = 1.0 / jnp.maximum(fold_ref[...], 1.0)

    def three(own, rim):
        up = pltpu.roll(jnp.where(sub == mids - 1, rim, own), 1, 0)
        down = pltpu.roll(jnp.where(sub == 0, rim, own), mids - 1, 0)
        return own + up + down

    def stack(gb, _):
        g, b = gb // blocks, gb % blocks
        total = jnp.zeros(shape, jnp.float32)
        square = jnp.zeros(shape, jnp.float32)
        rim_total = jnp.zeros(shape, jnp.float32)
        rim_square = jnp.zeros(shape, jnp.float32)
        for h in range(classes):
            row = (g * classes + h) * blocks + b
            start = start_ref[row]
            first = pl.multiple_of((start // LANES) * LANES, LANES)
            second = pl.multiple_of(first + LANES, LANES)
            offset = start % LANES
            low_mask = lane >= offset
            high_mask = lane > offset
            bc = lambda ref: jnp.broadcast_to(ref[pl.ds(row, 1), :], shape)
            li, hi, lw, hw = bc(low_at), bc(high_at), bc(low_w), bc(high_w)
            for at, is_rim in ((0, False), (mids, True)):
                near = x_ref[h, at:at + mids, pl.ds(first, LANES)]
                far = x_ref[h, at:at + mids, pl.ds(second, LANES)]
                moved = lw * take_lanes(jnp.where(low_mask, near, far), li) + hw * take_lanes(
                    jnp.where(high_mask, near, far), hi
                )
                if is_rim:
                    rim_total += moved
                    rim_square += moved * moved
                else:
                    total += moved
                    square += moved * moved
        rows = pl.ds(pl.multiple_of(g * mids, mids), mids)
        shifted = pl.ds(pl.multiple_of(b * LANES + LANES, LANES), LANES)
        sums[b, rows, :] = total * scale
        power[rows, shifted] = three(total * total, rim_total * rim_total)
        energy[rows, shifted] = three(square, rim_square)
        return 0

    lax.fori_loop(0, vels * blocks, stack, 0)

    width = samples + 2 * LANES

    def window(plane):
        by3 = plane + pltpu.roll(plane, 1, 1) + pltpu.roll(plane, width - 1, 1)
        by9 = by3 + pltpu.roll(by3, 3, 1) + pltpu.roll(by3, width - 3, 1)
        return by9[:, LANES:LANES + samples]

    def finish(g, _):
        rows = pl.ds(pl.multiple_of(g * mids, mids), mids)
        top = window(power[rows, :])
        bottom = window(energy[rows, :])
        value = top / jnp.maximum(classes * bottom, 1.0)
        for b in range(blocks):
            ratio[b, rows, :] = value[:, b * LANES:(b + 1) * LANES]
        return 0

    lax.fori_loop(0, vels, finish, 0)

    def turn(b, _):
        columns = pl.ds(pl.multiple_of(b * LANES, LANES), LANES)
        for m in range(mids):
            for half in range(vels // GROUP):
                semblance_ref[m, half * GROUP:(half + 1) * GROUP, columns] = ratio[
                    b, pl.ds(half * GROUP * mids + m, GROUP, stride=mids), :]
            stacked_ref[m, :, columns] = jnp.concatenate([
                sums[b, pl.ds(half * GROUP * mids + m, GROUP, stride=mids), :]
                for half in range(vels // GROUP)
            ], axis=0).astype(jnp.bfloat16)
        return 0

    lax.fori_loop(0, blocks, turn, 0)


def panels(x, fold, offsets, velocities, samples):
    classes, rows, _ = x.shape
    mids = rows // 2
    vels = velocities.shape[0]
    blocks = samples // LANES
    slowness = offsets[None, :] / velocities[:, None]
    slow = slowness * slowness
    time = (jnp.arange(blocks) * LANES).astype(jnp.float32)
    position = jnp.sqrt(time * time + slow[:, :, None])
    start = jnp.minimum(jnp.floor(position), float(samples)).astype(jnp.int32).reshape(-1)
    smem = pl.BlockSpec(memory_space=pltpu.SMEM)
    vmem = pl.BlockSpec(memory_space=pltpu.VMEM)
    count = vels * classes * blocks
    return pl.pallas_call(
        panels_kernel,
        out_shape=(
            jax.ShapeDtypeStruct((mids, vels, samples), jnp.bfloat16),
            jax.ShapeDtypeStruct((mids, vels, samples), jnp.float32),
        ),
        in_specs=[smem, smem, vmem, vmem],
        out_specs=(vmem, vmem),
        scratch_shapes=[
            pltpu.VMEM((count, LANES), jnp.int32),
            pltpu.VMEM((count, LANES), jnp.int32),
            pltpu.VMEM((count, LANES), jnp.float32),
            pltpu.VMEM((count, LANES), jnp.float32),
            pltpu.VMEM((vels * mids, samples + 2 * LANES), jnp.float32),
            pltpu.VMEM((vels * mids, samples + 2 * LANES), jnp.float32),
            pltpu.VMEM((blocks, vels * mids, LANES), jnp.float32),
            pltpu.VMEM((blocks, vels * mids, LANES), jnp.float32),
        ],
        name="panels",
    )(start, slow.reshape(-1), x, fold)


def per_device(traces, owners, midpoint, offset_class, offsets, velocities):
    inline_count = lax.axis_size("inline")
    xline_count = lax.axis_size("xline")
    devices = inline_count * xline_count
    axes = ("inline", "xline")
    me = lax.axis_index(axes)
    trace_rows, samples = traces.shape
    classes = offsets.shape[0]
    capacity = max(2, 2 * trace_rows // devices)
    target = owners[:, 0]
    onehot_dest = (target[:, None] == jnp.arange(devices)[None, :]).astype(jnp.int32)
    slot_rank = jnp.sum((jnp.cumsum(onehot_dest, axis=0) - onehot_dest) * onehot_dest, axis=1)
    slot_row = target * capacity + slot_rank
    buffer = jnp.zeros((devices * capacity, samples), traces.dtype).at[slot_row].set(traces)
    slot_keys = (
        jnp.full((devices * capacity,), -1, jnp.int32)
        .at[slot_row]
        .set(offset_class * CMP_DEV + midpoint)
    )
    buffer = buffer.reshape(inline_count, xline_count, capacity, samples)
    slot_keys = slot_keys.reshape(inline_count, xline_count, capacity)

    def exchange(block):
        block = lax.all_to_all(block, "inline", split_axis=0, concat_axis=0, tiled=True)
        return lax.all_to_all(block, "xline", split_axis=1, concat_axis=1, tiled=True)

    arrived_keys = exchange(slot_keys).reshape(-1)
    arrived = exchange(buffer).reshape(-1, samples)
    members = arrived_keys[None, :] == jnp.arange(classes * CMP_DEV)[:, None]
    gathers = jnp.dot(members.astype(jnp.bfloat16), arrived, preferred_element_type=jnp.float32)
    binned = gathers.astype(jnp.bfloat16).reshape(classes, CMP_DEV, samples)
    counts = jnp.sum(members.astype(jnp.float32), axis=1).reshape(classes, CMP_DEV)
    fold = jnp.broadcast_to(jnp.sum(counts, axis=0)[:, None], (CMP_DEV, LANES))
    forward = [(i, i + 1) for i in range(devices - 1)]
    backward = [(i + 1, i) for i in range(devices - 1)]
    left = lax.ppermute(binned[:, CMP_DEV - 1:], axes, forward)
    right = lax.ppermute(binned[:, :1], axes, backward)
    middle = jnp.zeros((classes, CMP_DEV - 2, samples), binned.dtype)
    x = jnp.concatenate([binned, right, middle, left], axis=1).astype(jnp.float32)
    x = jnp.pad(x, ((0, 0), (0, 0), (0, 2 * LANES)))
    return panels(x, fold, offsets, velocities, samples)


def solution(mesh):
    in_specs = (
        P(("inline", "xline"), None),
        P(("inline", "xline"), None),
        P(("inline", "xline")),
        P(("inline", "xline")),
        P(),
        P(),
    )
    out_specs = (P(("inline", "xline"), None, None), P(("inline", "xline"), None, None))
    return jax.shard_map(
        per_device, mesh=mesh, in_specs=in_specs, out_specs=out_specs, check_vma=False
    )
```

time: 444 us -> 185 us (0.42); the launches traced: 435 us -> 184 us
  local copies, waits for them, and re-layouts: 202 us -> 22 us
  blocking collectives: 88.8 us -> 0 us
  waiting for transfers between devices: 37.5 us -> 84.7 us
  Pallas kernels: 0 us -> 40.1 us
  matrix products: 40.4 us -> 0.45 us
  loops' own time: 16.5 us -> 0 us
  other arithmetic: 15.8 us -> 3.8 us
    gather x8 -> x0, local copies, waits for them, and re-layouts: 171 us -> none  [cut_window(): return lax.dynamic_slice_in_dim(plane_rows, start_at, window_len, 1)]
    unnamed x1 -> x0, blocking collectives: 88.8 us -> none
    all_to_all x4, waiting for transfers between devices: 32.2 us -> 81.9 us  [the longest x2 53.1 us: exchange(): lax.all_to_all(block, 'xline', split_axis=1, concat_axis=1, tiled=True)]
    pallas_call x0 -> x1, Pallas kernels: none -> 40.1 us  [panels(): pl.pallas_call(panels_kernel, out_shape=(jax.ShapeDtypeStruct((mids, vels...]
    dot_general x4 -> x0, matrix products: 39.9 us -> none  [per_group(): jnp.einsum('ghbmr,ghbrq->gmhbq', windows, weights, preferred_element_type...]
    another operation x1 -> x0, loops' own time: 16.5 us -> none  [panels(): summed, energy = lax.map(per_group, velocities.reshape(-1, vel_group))]
    another operation x7 -> x3, other arithmetic: 4.76 us -> 0.26 us  [the longest x2 4.5 us: per_device(): planes = jnp.stack([window_sum(summed * summed), window_sum(energy)])]
  transfers between devices with their start and end apart: 6 -> 6, of which waited for: 5 -> 5; matrix products, arithmetic and copies ran while one was open for 3% -> 7% of each run, Pallas kernels for 0% -> 0%
where the time goes in v1:
time: 185 us; the launch traced here: 184 us
  waiting for transfers between devices  84.7 us (46%)
  Pallas kernels  40.1 us (22%)
  starting transfers between devices  31.9 us (17%)
  local copies, waits for them, and re-layouts  22 us (12%)
  other arithmetic  3.8 us (2%)
    all_to_all x2, waiting for transfers between devices, exchange(): lax.all_to_all(block, 'xline', split_axis=1, concat_axis=1, tiled=True)  53.1 us
    pallas_call x1, Pallas kernels, panels(): pl.pallas_call(panels_kernel, out_shape=(jax.ShapeDtypeStruct((mids, vels...  40.1 us
    all_to_all x2, waiting for transfers between devices, exchange(): lax.all_to_all(block, 'inline', split_axis=0, concat_axis=0, tiled=True)  28.8 us
    all_to_all x2, starting transfers between devices, exchange(): lax.all_to_all(block, 'inline', split_axis=0, concat_axis=0, tiled=True)  14.9 us
    all_to_all x2, starting transfers between devices, exchange(): lax.all_to_all(block, 'xline', split_axis=1, concat_axis=1, tiled=True)  11.8 us
    all_to_all x2, local copies, waits for them, and re-layouts, exchange(): lax.all_to_all(block, 'inline', split_axis=0, concat_axis=0, tiled=True)  3.81 us
    all_to_all x2, local copies, waits for them, and re-layouts, exchange(): lax.all_to_all(block, 'xline', split_axis=1, concat_axis=1, tiled=True)  3.76 us
  transfers between devices with their start and end apart: 6, of which 5 were waited for; matrix products, arithmetic and copies ran while one was open for 7% of the time, Pallas kernels for 0%

profile of v1, /device:TPU:1, one launch (start us, length us, event | category | flops | bytes accessed | tf_op | source)
XLA Modules:
  0.0 183.9 jit_solution(12286445940853514688)
XLA Ops:
  0.6 0.8 copy.31
  1.7 0.9 fusion.5
  2.6 0.7 compare_select_fusion
  3.3 0.7 multiply_add_fusion
  4.0 1.4 scatter_custom_fusion
  5.5 0.9 copy.33
  6.4 8.6 %all-to-all-start = ((s32[32,8,2]{1,2,0:T(2,128)}), s32[32,8,2]{1,2,0:T(2,128)S(1)}, u32[]{:S(2)}, u32[]{:S(2)}) async-start(s32[32,8,2]{1,2,0:T(2,128)} %copy.33), calls=%async_computation | async-start | bytes 65536 | tf_op jit(solution)/shard_map/all_to_all | solution.py:189
  15.0 3.5 %scatter_custom_fusion.1 = bf16[512,2048]{1,0:T(8,128)(2,1)S(1)} fusion(s32[256]{0:T(256)S(1)} %bitcast.27, bf16[256,2048]{1,0:T(8,128)(2,1)} %param.6, bf16[]{:T(256)} %constant.24.clone.1), kind=kCustom, calls=%fused_computation.4 | custom fusion | bytes 2097664 | tf_op jit(solution)/shard_map/scatter | solution.py:179
  18.5 2.7 %reshape.87 = bf16[32,8,2,2048]{3,2,1,0:T(2,128)(2,1)} reshape(bf16[512,2048]{1,0:T(8,128)(2,1)S(1)} %scatter_custom_fusion.1) | data formatting | bytes 4194304 | tf_op jit(solution)/shard_map/reshape | solution.py:185
  21.2 1.1 all-to-all-done
  22.3 6.3 %all-to-all-start.2 = ((bf16[32,8,2,2048]{3,2,1,0:T(2,128)(2,1)}), bf16[32,8,2,2048]{3,2,1,0:T(2,128)(2,1)S(1)}, u32[]{:S(2)}, u32[]{:S(2)}) async-start(bf16[32,8,2,2048]{3,2,1,0:T(2,128)(2,1)} %reshape.87), calls=%async_computation.2 | async-start | bytes 4194304 | tf_op jit(solution)/shard_map/all_to_all | solution.py:189
  29.2 27.7 %all-to-all-done.2 = bf16[32,8,2,2048]{3,2,1,0:T(2,128)(2,1)S(1)} async-done(((bf16[32,8,2,2048]{3,2,1,0:T(2,128)(2,1)}), bf16[32,8,2,2048]{3,2,1,0:T(2,128)(2,1)S(1)}, u32[]{:S(2)}, u32[]{:S(2)}) %all-to-all-start.2) | async-done | bytes 2097184 | tf_op jit(solution)/shard_map/all_to_all | solution.py:189
  56.9 8.2 %all-to-all-start.1 = ((s32[32,8,2]{0,2,1:T(2,128)}), s32[32,8,2]{0,2,1:T(2,128)S(1)}, u32[]{:S(2)}, u32[]{:S(2)}) async-start(s32[32,8,2]{0,2,1:T(2,128)} %copy.34), calls=%async_computation.1 | async-start | bytes 16384 | tf_op jit(solution)/shard_map/all_to_all | solution.py:190
  65.1 3.1 %copy.36 = bf16[32,8,2,2048]{3,2,0,1:T(2,128)(2,1)} copy(bf16[32,8,2,2048]{3,2,1,0:T(2,128)(2,1)S(1)} %all-to-all-done.2) | data formatting | bytes 4194304 | tf_op jit(solution)/shard_map/all_to_all | solution.py:189
  68.2 3.4 %all-to-all-done.1 = s32[32,8,2]{0,2,1:T(2,128)S(1)} async-done(((s32[32,8,2]{0,2,1:T(2,128)}), s32[32,8,2]{0,2,1:T(2,128)S(1)}, u32[]{:S(2)}, u32[]{:S(2)}) %all-to-all-start.1) | async-done | bytes 2080 | tf_op jit(solution)/shard_map/all_to_all | solution.py:190
  71.7 3.6 %all-to-all-start.3 = ((bf16[32,8,2,2048]{3,2,0,1:T(2,128)(2,1)}), bf16[32,8,2,2048]{3,2,0,1:T(2,128)(2,1)S(1)}, u32[]{:S(2)}, u32[]{:S(2)}) async-start(bf16[32,8,2,2048]{3,2,0,1:T(2,128)(2,1)} %copy.36), calls=%async_computation.3 | async-start | bytes 4194304 | tf_op jit(solution)/shard_map/all_to_all | solution.py:190
  77.2 49.7 %all-to-all-done.3 = bf16[32,8,2,2048]{3,2,0,1:T(2,128)(2,1)S(1)} async-done(((bf16[32,8,2,2048]{3,2,0,1:T(2,128)(2,1)}), bf16[32,8,2,2048]{3,2,0,1:T(2,128)(2,1)S(1)}, u32[]{:S(2)}, u32[]{:S(2)}) %all-to-all-start.3) | async-done | bytes 2097184 | tf_op jit(solution)/shard_map/all_to_all | solution.py:190
  126.9 3.6 %copy.37 = bf16[32,8,2,2048]{3,2,1,0:T(2,128)(2,1)} copy(bf16[32,8,2,2048]{3,2,0,1:T(2,128)(2,1)S(1)} %all-to-all-done.3) | data formatting | bytes 4194304 | tf_op jit(solution)/shard_map/all_to_all | solution.py:190
  130.5 2.7 %reshape.88 = bf16[512,2048]{1,0:T(8,128)(2,1)S(1)} reshape(bf16[32,8,2,2048]{3,2,1,0:T(2,128)(2,1)} %copy.37) | data formatting | bytes 4194304 | tf_op jit(solution)/shard_map/reshape | solution.py:193
  133.7 1.9 %collective-permute-start = (bf16[4,1,2048]{2,1,0:T(2,128)(2,1)S(1)}, bf16[4,1,2048]{2,1,0:T(2,128)(2,1)S(1)}, u32[]{:S(2)}, u32[]{:S(2)}) collective-permute-start(bf16[4,1,2048]{2,1,0:T(2,128)(2,1)S(1)} %get-tuple-element.2), channel_id=1, source_target_pairs={{1,0},{2,1},{3,2},{4,3},{5,4},{6,5},{7,6},{8,7},{9,8},{10,9},{11,1... | collective-permute-start | bytes 49160 | tf_op jit(solution)/shard_map/ppermute | solution.py:202
  135.7 3.4 %collective-permute-start.1 = (bf16[4,1,2048]{2,1,0:T(2,128)(2,1)S(1)}, bf16[4,1,2048]{2,1,0:T(2,128)(2,1)S(1)}, u32[]{:S(2)}, u32[]{:S(2)}) collective-permute-start(bf16[4,1,2048]{2,1,0:T(2,128)(2,1)S(1)} %get-tuple-element.3), channel_id=1, source_target_pairs={{0,1},{1,2},{2,3},{3,4},{4,5},{5,6},{6,7},{7,8},{8,9},{9,10},{10,1... | collective-permute-start | bytes 49160 | tf_op jit(solution)/shard_map/ppermute | solution.py:201
  139.3 2.8 %collective-permute-done.1 = bf16[4,1,2048]{2,1,0:T(2,128)(2,1)S(1)} collective-permute-done((bf16[4,1,2048]{2,1,0:T(2,128)(2,1)S(1)}, bf16[4,1,2048]{2,1,0:T(2,128)(2,1)S(1)}, u32[]{:S(2)}, u32[]{:S(2)}) %collective-permute-start.1) | collective-permute-done | bytes 16416 | tf_op jit(solution)/shard_map/ppermute | solution.py:201
  142.2 0.8 pad_convert_fusion.x_ref
  143.8 40.1 %panels.1 = (bf16[8,16,2048]{2,1,0:T(8,128)(2,1)}, f32[8,16,2048]{2,1,0:T(8,128)}) custom-call(s32[1024]{0:T(1024)} %reshape.91.start_ref, f32[64]{0:T(128)} %mul.44.slow_ref, f32[4,16,2304]{2,1,0:T(8,128)} %pad_convert_fusion.x_ref, f32[8,128]{1,0:T(8,128)} %broadcast_in_dim.11.fold_ref), custom_call_target="tpu_custom_call" | custom-call | tf_op jit(solution)/shard_map/panels/pallas_call | solution.py:144
  (30 shorter events, 4.5 us)
Async XLA Ops:
  6.4 15.9 %all-to-all-start = ((s32[32,8,2]{1,2,0:T(2,128)}), s32[32,8,2]{1,2,0:T(2,128)S(1)}, u32[]{:S(2)}, u32[]{:S(2)}) async-start(s32[32,8,2]{1,2,0:T(2,128)} %copy.33), calls=%async_computation | async-start | bytes 65536 | tf_op jit(solution)/shard_map/all_to_all | solution.py:189
  22.3 34.6 %all-to-all-start.2 = ((bf16[32,8,2,2048]{3,2,1,0:T(2,128)(2,1)}), bf16[32,8,2,2048]{3,2,1,0:T(2,128)(2,1)S(1)}, u32[]{:S(2)}, u32[]{:S(2)}) async-start(bf16[32,8,2,2048]{3,2,1,0:T(2,128)(2,1)} %reshape.87), calls=%async_computation.2 | async-start | bytes 4194304 | tf_op jit(solution)/shard_map/all_to_all | solution.py:189
  56.9 14.8 %all-to-all-start.1 = ((s32[32,8,2]{0,2,1:T(2,128)}), s32[32,8,2]{0,2,1:T(2,128)S(1)}, u32[]{:S(2)}, u32[]{:S(2)}) async-start(s32[32,8,2]{0,2,1:T(2,128)} %copy.34), calls=%async_computation.1 | async-start | bytes 16384 | tf_op jit(solution)/shard_map/all_to_all | solution.py:190
  68.2 7.1 %copy-start = (f32[16]{0:T(128)S(1)}, f32[16]{0:T(128)}, u32[]{:S(2)}) copy-start(f32[16]{0:T(128)} %param.11) | copy-start | bytes 196
  68.2 7.1 %copy-start.1 = (f32[4]{0:T(128)S(1)}, f32[4]{0:T(128)}, u32[]{:S(2)}) copy-start(f32[4]{0:T(128)} %param.10) | copy-start | bytes 52
  71.7 55.2 %all-to-all-start.3 = ((bf16[32,8,2,2048]{3,2,0,1:T(2,128)(2,1)}), bf16[32,8,2,2048]{3,2,0,1:T(2,128)(2,1)S(1)}, u32[]{:S(2)}, u32[]{:S(2)}) async-start(bf16[32,8,2,2048]{3,2,0,1:T(2,128)(2,1)} %copy.36), calls=%async_computation.3 | async-start | bytes 4194304 | tf_op jit(solution)/shard_map/all_to_all | solution.py:190
  133.7 5.5 %collective-permute-start = (bf16[4,1,2048]{2,1,0:T(2,128)(2,1)S(1)}, bf16[4,1,2048]{2,1,0:T(2,128)(2,1)S(1)}, u32[]{:S(2)}, u32[]{:S(2)}) collective-permute-start(bf16[4,1,2048]{2,1,0:T(2,128)(2,1)S(1)} %get-tuple-element.2), channel_id=1, source_target_pairs={{1,0},{2,1},{3,2},{4,3},{5,4},{6,5},{7,6},{8,7},{9,8},{10,9},{11,1... | collective-permute-start | bytes 49160 | tf_op jit(solution)/shard_map/ppermute | solution.py:202
  135.7 6.4 %collective-permute-start.1 = (bf16[4,1,2048]{2,1,0:T(2,128)(2,1)S(1)}, bf16[4,1,2048]{2,1,0:T(2,128)(2,1)S(1)}, u32[]{:S(2)}, u32[]{:S(2)}) collective-permute-start(bf16[4,1,2048]{2,1,0:T(2,128)(2,1)S(1)} %get-tuple-element.3), channel_id=1, source_target_pairs={{0,1},{1,2},{2,3},{3,4},{4,5},{5,6},{6,7},{7,8},{8,9},{9,10},{10,1... | collective-permute-start | bytes 49160 | tf_op jit(solution)/shard_map/ppermute | solution.py:201

commit v2 on v1

--- a/solution.py
+++ b/solution.py
@@ -25,7 +25,12 @@
     classes = x_ref.shape[0]
     blocks = samples // LANES
 
-    def prepare(gh, _):
+    def prepare(step, _):
+        for part in range(4):
+            prepare_one(step * 4 + part)
+        return 0
+
+    def prepare_one(gh):
         row = lax.broadcasted_iota(jnp.int32, (blocks, LANES), 0)
         lane = lax.broadcasted_iota(jnp.int32, (blocks, LANES), 1)
         time = (row * LANES + lane).astype(jnp.float32)
@@ -38,9 +43,8 @@
         high_at[rows, :] = (index + 1) & (LANES - 1)
         low_w[rows, :] = (1.0 - fraction).astype(jnp.bfloat16).astype(jnp.float32)
         high_w[rows, :] = fraction.astype(jnp.bfloat16).astype(jnp.float32)
-        return 0
-
-    lax.fori_loop(0, vels * classes, prepare, 0)
+
+    lax.fori_loop(0, vels * classes // 4, prepare, 0)
 
     edge = jnp.zeros((mids, LANES), jnp.float32)
     for g in range(vels):
@@ -58,8 +62,13 @@
         down = pltpu.roll(jnp.where(sub == 0, rim, own), mids - 1, 0)
         return own + up + down
 
-    def stack(gb, _):
-        g, b = gb // blocks, gb % blocks
+    def stack(step, _):
+        g = step >> 2
+        for part in range(blocks // 4):
+            stack_one(g, (step & 3) * (blocks // 4) + part)
+        return 0
+
+    def stack_one(g, b):
         total = jnp.zeros(shape, jnp.float32)
         square = jnp.zeros(shape, jnp.float32)
         rim_total = jnp.zeros(shape, jnp.float32)
@@ -67,9 +76,9 @@
         for h in range(classes):
             row = (g * classes + h) * blocks + b
             start = start_ref[row]
-            first = pl.multiple_of((start // LANES) * LANES, LANES)
+            first = pl.multiple_of((start >> 7) << 7, LANES)
             second = pl.multiple_of(first + LANES, LANES)
-            offset = start % LANES
+            offset = start & (LANES - 1)
             low_mask = lane >= offset
             high_mask = lane > offset
             bc = lambda ref: jnp.broadcast_to(ref[pl.ds(row, 1), :], shape)
@@ -91,9 +100,8 @@
         sums[b, rows, :] = total * scale
         power[rows, shifted] = three(total * total, rim_total * rim_total)
         energy[rows, shifted] = three(square, rim_square)
-        return 0
-
-    lax.fori_loop(0, vels * blocks, stack, 0)
+
+    lax.fori_loop(0, vels * 4, stack, 0)
 
     width = samples + 2 * LANES
 
@@ -162,47 +170,292 @@
         name="panels",
     )(start, slow.reshape(-1), x, fold)
 
+MESH = pl.DeviceIdType.MESH
+CHUNKS = 4
+TILE = 256
+
+
+def gather_kernel(
+    dims, traces_ref, owner_ref, key_ref, x_ref, fold_ref,
+    buf, arr, kout, karr, member, zout, zarr, cout, carr, eout, earr,
+    plane_send, plane_recv, zed_send, zed_recv, rim_send, rim_recv, own_sem,
+):
+    nx, ny, nz = dims
+    inline = nx * ny * 2
+    rows, samples = traces_ref.shape
+    slots = buf.shape[0] // inline
+    bins = zout.shape[1]
+    classes = x_ref.shape[0]
+    mids = bins // classes
+    width = samples // CHUNKS
+    tile = min(TILE, width)
+    me, mz = lax.axis_index("inline"), lax.axis_index("xline")
+    mx, my, mc = me // (2 * ny), (me // 2) % ny, me % 2
+
+    def plane_peer(p, sign):
+        q = p // 2
+        dx = q % nx
+        dy = (q // nx + dx) % ny
+        px = (mx + nx + sign * dx) % nx
+        py = (my + ny + sign * dy) % ny
+        return (px * ny + py) * 2 + (mc + p) % 2
+
+    def zed_peer(p):
+        step = (p + 1) // 2
+        return (mz + jnp.where(p % 2 == 1, step, nz - step)) % nz
+
+    right = (lax.rem(me + jnp.where(mz == nz - 1, 1, 0), inline), lax.rem(mz + 1, nz))
+    left = (lax.rem(me + jnp.where(mz == 0, inline - 1, 0), inline), lax.rem(mz + nz - 1, nz))
+
+    barrier = pltpu.get_barrier_semaphore()
+
+    def greet_plane(p, _):
+        pl.semaphore_signal(barrier, inc=1, device_id=(plane_peer(p, 1), mz), device_id_type=MESH)
+        return 0
+
+    def greet_zed(p, _):
+        pl.semaphore_signal(barrier, inc=1, device_id=(me, zed_peer(p)), device_id_type=MESH)
+        return 0
+
+    lax.fori_loop(1, inline, greet_plane, 0)
+    lax.fori_loop(1, nz, greet_zed, 0)
+    for peer in (left, right):
+        pl.semaphore_signal(barrier, inc=1, device_id=peer, device_id_type=MESH)
+
+    square = (rows, rows)
+    first = lax.broadcasted_iota(jnp.int32, square, 0)
+    second = lax.broadcasted_iota(jnp.int32, square, 1)
+    owner_row = owner_ref[...]
+    owner_all = jnp.broadcast_to(owner_row.astype(jnp.float32), square)
+    owner_col = jnp.sum(jnp.where(first == second, owner_all, 0.0), axis=1, keepdims=True)
+    same = owner_all == owner_col
+    rank_row = jnp.sum(jnp.where(same & (first < second), 1.0, 0.0), axis=0, keepdims=True).astype(jnp.int32)
+    rank_col = jnp.sum(jnp.where(same & (second < first), 1.0, 0.0), axis=1, keepdims=True).astype(jnp.int32)
+    capacity = slots // nz
+    slot_row = owner_row * capacity + rank_row
+    wide = (buf.shape[0], rows)
+    member_out = jnp.where(
+        lax.broadcasted_iota(jnp.int32, wide, 0) == slot_row, 1.0, 0.0).astype(jnp.bfloat16)
+    per_lane = 128 // slots
+    owner_col = owner_col.astype(jnp.int32)
+    lane_at = (me % per_lane) * slots + (owner_col % nz) * capacity + rank_col
+    placed = jnp.where(
+        lax.broadcasted_iota(jnp.int32, (rows, 128), 1) == lane_at, 1.0, 0.0).astype(jnp.bfloat16)
+    number = ((owner_row % nz) * bins + key_ref[...] + 1).astype(jnp.float32)
+    chosen = jnp.where(
+        lax.broadcasted_iota(jnp.int32, (inline, rows), 0) == owner_row // nz, number, 0.0
+    ).astype(jnp.bfloat16)
+    keys = jnp.dot(chosen, placed, preferred_element_type=jnp.float32)
+    for i in range(inline):
+        kout[i] = keys[i:i + 1, :]
+    member[0:buf.shape[0], 0:rows] = member_out
+
+    def place(t, _):
+        columns = pl.ds(pl.multiple_of(t * tile, tile), tile)
+        buf[:, columns] = jnp.dot(
+            member[0:buf.shape[0], 0:rows], traces_ref[:, columns],
+            preferred_element_type=jnp.float32).astype(jnp.bfloat16)
+        return 0
+
+    lax.fori_loop(0, samples // tile, place, 0)
+
+    pl.semaphore_wait(barrier, inline - 1 + nz - 1 + 2)
+
+    own = pl.ds(pl.multiple_of(me * slots, slots), slots)
+    own_copy = pltpu.make_async_copy(buf.at[own, :], arr.at[own, :], own_sem)
+    own_copy.start()
+
+    def send_key(p, _):
+        peer = plane_peer(p, 1)
+        pltpu.make_async_remote_copy(
+            src_ref=kout.at[peer], dst_ref=karr.at[me],
+            send_sem=plane_send.at[CHUNKS], recv_sem=plane_recv.at[CHUNKS],
+            device_id=(peer, mz), device_id_type=MESH).start()
+        return 0
+
+    lax.fori_loop(1, inline, send_key, 0)
+
+    def cut(c):
+        return pl.ds(c * width, width)
+
+    for c in range(CHUNKS):
+        def send_plane(p, _, c=c):
+            peer = plane_peer(p, 1)
+            pltpu.make_async_remote_copy(
+                src_ref=buf.at[pl.ds(pl.multiple_of(peer * slots, slots), slots), cut(c)],
+                dst_ref=arr.at[own, cut(c)],
+                send_sem=plane_send.at[c], recv_sem=plane_recv.at[c],
+                device_id=(peer, mz), device_id_type=MESH).start()
+            return 0
+        lax.fori_loop(1, inline, send_plane, 0)
+
+    def all_of(ref, sem):
+        pltpu.make_async_copy(ref, ref, sem).wait()
+
+    karr[me] = kout[me]
+    all_of(karr.at[pl.ds(0, inline - 1)], plane_recv.at[CHUNKS])
+    for q in range(inline // per_lane):
+        line = karr[q * per_lane]
+        for s in range(1, per_lane):
+            line = line + karr[q * per_lane + s]
+        number_at = lax.broadcasted_iota(jnp.int32, (nz * bins, 128), 0) + 1
+        member[0:nz * bins, q * 128:(q + 1) * 128] = jnp.where(
+            line.astype(jnp.int32) == number_at, 1.0, 0.0).astype(jnp.bfloat16)
+    arrived_rows = inline * slots
+    counts = jnp.dot(
+        member[0:nz * bins, 0:arrived_rows], jnp.ones((arrived_rows, 128), jnp.bfloat16),
+        preferred_element_type=jnp.float32)
+    for z in range(nz):
+        cout[z] = counts[z * bins:(z + 1) * bins]
+    carr[mz] = cout[mz]
+
+    def send_count(p, _):
+        peer = zed_peer(p)
+        pltpu.make_async_remote_copy(
+            src_ref=cout.at[peer], dst_ref=carr.at[mz],
+            send_sem=zed_send.at[CHUNKS], recv_sem=zed_recv.at[CHUNKS],
+            device_id=(me, peer), device_id_type=MESH).start()
+        return 0
+
+    own_copy.wait()
+
+    def bin_chunk(c):
+        all_of(arr.at[pl.ds(0, (inline - 1) * slots), cut(c)], plane_recv.at[c])
+
+        def bin_tile(t, _):
+            columns = pl.ds(pl.multiple_of(c * width + t * tile, tile), tile)
+            part = jnp.dot(
+                member[0:nz * bins, 0:arrived_rows], arr[:, columns],
+                preferred_element_type=jnp.float32).astype(jnp.bfloat16)
+            for z in range(nz):
+                zout[z, :, columns] = part[z * bins:(z + 1) * bins]
+            return 0
+
+        lax.fori_loop(0, width // tile, bin_tile, 0)
+        zarr[mz, :, cut(c)] = zout[mz, :, cut(c)]
+        if c == 0:
+            lax.fori_loop(1, nz, send_count, 0)
+
+        def send_zed(p, _):
+            peer = zed_peer(p)
+            pltpu.make_async_remote_copy(
+                src_ref=zout.at[peer, :, cut(c)], dst_ref=zarr.at[mz, :, cut(c)],
+                send_sem=zed_send.at[c], recv_sem=zed_recv.at[c],
+                device_id=(me, peer), device_id_type=MESH).start()
+            return 0
+
+        lax.fori_loop(1, nz, send_zed, 0)
+
+    def rim_copies(c):
+        return [pltpu.make_async_remote_copy(
+            src_ref=eout.at[side, :, cut(c)], dst_ref=earr.at[side, :, cut(c)],
+            send_sem=rim_send.at[side, c], recv_sem=rim_recv.at[side, c],
+            device_id=peer, device_id_type=MESH) for side, peer in ((0, left), (1, right))]
+
+    def sum_chunk(c):
+        all_of(zarr.at[pl.ds(0, nz - 1), :, cut(c)], zed_recv.at[c])
+
+        def sum_tile(t, _):
+            columns = pl.ds(pl.multiple_of(c * width + t * 128, 128), 128)
+            total = zarr[0, :, columns].astype(jnp.float32)
+            for z in range(1, nz):
+                total = total + zarr[z, :, columns].astype(jnp.float32)
+            total = total.astype(jnp.bfloat16).astype(jnp.float32)
+            for h in range(classes):
+                part = total[h * mids:(h + 1) * mids]
+                x_ref[h, 0:mids, columns] = part
+                eout[0, h:h + 1, columns] = part[0:1]
+                eout[1, h:h + 1, columns] = part[mids - 1:mids]
+            return 0
+
+        lax.fori_loop(0, width // 128, sum_tile, 0)
+        for copy in rim_copies(c):
+            copy.start()
+
+    for c in range(CHUNKS + 1):
+        if c < CHUNKS:
+            bin_chunk(c)
+        if c >= 1:
+            sum_chunk(c - 1)
+
+    all_of(carr.at[pl.ds(0, nz - 1)], zed_recv.at[CHUNKS])
+    total = carr[0]
+    for z in range(1, nz):
+        total = total + carr[z]
+    fold = total[0:mids]
+    for h in range(1, classes):
+        fold = fold + total[h * mids:(h + 1) * mids]
+    fold_ref[...] = fold
+
+    for h in range(classes):
+        x_ref[h, :, samples:] = jnp.zeros((2 * mids, x_ref.shape[2] - samples), jnp.float32)
+        x_ref[h, mids:, 0:samples] = jnp.zeros((mids, samples), jnp.float32)
+    for c in range(CHUNKS):
+        for copy in rim_copies(c):
+            copy.wait()
+    is_first = (me == 0) & (mz == 0)
+    is_last = (me == inline - 1) & (mz == nz - 1)
+    for h in range(classes):
+        from_right, from_left = earr[0, h:h + 1, :], earr[1, h:h + 1, :]
+        x_ref[h, mids:mids + 1, 0:samples] = jnp.where(is_last, jnp.zeros_like(from_right), from_right)
+        x_ref[h, 2 * mids - 1:2 * mids, 0:samples] = jnp.where(is_first, jnp.zeros_like(from_left), from_left)
+
+    for c in range(CHUNKS):
+        all_of(buf.at[pl.ds(0, (inline - 1) * slots), cut(c)], plane_send.at[c])
+        all_of(zout.at[pl.ds(0, nz - 1), :, cut(c)], zed_send.at[c])
+    all_of(kout.at[pl.ds(0, inline - 1)], plane_send.at[CHUNKS])
+    all_of(cout.at[pl.ds(0, nz - 1)], zed_send.at[CHUNKS])
+
+
+def gather(dims, traces, owners, keys, classes, mids):
+    nx, ny, nz = dims
+    inline = nx * ny * 2
+    rows, samples = traces.shape
+    capacity = max(2, 2 * rows // (inline * nz))
+    slots = nz * capacity
+    bins = classes * mids
+    f32, bf16 = jnp.float32, jnp.bfloat16
+    vmem = pl.BlockSpec(memory_space=pltpu.VMEM)
+    dma = pltpu.SemaphoreType.DMA
+    return pl.pallas_call(
+        functools.partial(gather_kernel, dims),
+        out_shape=(
+            jax.ShapeDtypeStruct((classes, 2 * mids, samples + 2 * LANES), f32),
+            jax.ShapeDtypeStruct((mids, LANES), f32),
+        ),
+        in_specs=[vmem] * 3,
+        out_specs=(vmem, vmem),
+        scratch_shapes=[
+            pltpu.VMEM((inline * slots, samples), bf16),
+            pltpu.VMEM((inline * slots, samples), bf16),
+            pltpu.VMEM((inline, 1, 128), f32),
+            pltpu.VMEM((inline, 1, 128), f32),
+            pltpu.VMEM((max(inline * slots, nz * bins), max(rows, inline * slots)), bf16),
+            pltpu.VMEM((nz, bins, samples), bf16),
+            pltpu.VMEM((nz, bins, samples), bf16),
+            pltpu.VMEM((nz, bins, 128), f32),
+            pltpu.VMEM((nz, bins, 128), f32),
+            pltpu.VMEM((2, classes, samples), f32),
+            pltpu.VMEM((2, classes, samples), f32),
+            dma((CHUNKS + 1,)), dma((CHUNKS + 1,)),
+            dma((CHUNKS + 1,)), dma((CHUNKS + 1,)),
+            dma((2, CHUNKS)), dma((2, CHUNKS)), dma,
+        ],
+        compiler_params=pltpu.CompilerParams(collective_id=0, has_side_effects=True),
+        name="gather",
+    )(traces, owners, keys)
+
 
 def per_device(traces, owners, midpoint, offset_class, offsets, velocities):
     inline_count = lax.axis_size("inline")
     xline_count = lax.axis_size("xline")
-    devices = inline_count * xline_count
-    axes = ("inline", "xline")
-    me = lax.axis_index(axes)
-    trace_rows, samples = traces.shape
+    side = round((inline_count // 2) ** 0.5)
     classes = offsets.shape[0]
-    capacity = max(2, 2 * trace_rows // devices)
-    target = owners[:, 0]
-    onehot_dest = (target[:, None] == jnp.arange(devices)[None, :]).astype(jnp.int32)
-    slot_rank = jnp.sum((jnp.cumsum(onehot_dest, axis=0) - onehot_dest) * onehot_dest, axis=1)
-    slot_row = target * capacity + slot_rank
-    buffer = jnp.zeros((devices * capacity, samples), traces.dtype).at[slot_row].set(traces)
-    slot_keys = (
-        jnp.full((devices * capacity,), -1, jnp.int32)
-        .at[slot_row]
-        .set(offset_class * CMP_DEV + midpoint)
+    rows, samples = traces.shape
+    keys = (offset_class * CMP_DEV + midpoint).reshape(1, rows)
+    x, fold = gather(
+        (side, side, xline_count), traces, owners.reshape(1, rows), keys, classes, CMP_DEV
     )
-    buffer = buffer.reshape(inline_count, xline_count, capacity, samples)
-    slot_keys = slot_keys.reshape(inline_count, xline_count, capacity)
-
-    def exchange(block):
-        block = lax.all_to_all(block, "inline", split_axis=0, concat_axis=0, tiled=True)
-        return lax.all_to_all(block, "xline", split_axis=1, concat_axis=1, tiled=True)
-
-    arrived_keys = exchange(slot_keys).reshape(-1)
-    arrived = exchange(buffer).reshape(-1, samples)
-    members = arrived_keys[None, :] == jnp.arange(classes * CMP_DEV)[:, None]
-    gathers = jnp.dot(members.astype(jnp.bfloat16), arrived, preferred_element_type=jnp.float32)
-    binned = gathers.astype(jnp.bfloat16).reshape(classes, CMP_DEV, samples)
-    counts = jnp.sum(members.astype(jnp.float32), axis=1).reshape(classes, CMP_DEV)
-    fold = jnp.broadcast_to(jnp.sum(counts, axis=0)[:, None], (CMP_DEV, LANES))
-    forward = [(i, i + 1) for i in range(devices - 1)]
-    backward = [(i + 1, i) for i in range(devices - 1)]
-    left = lax.ppermute(binned[:, CMP_DEV - 1:], axes, forward)
-    right = lax.ppermute(binned[:, :1], axes, backward)
-    middle = jnp.zeros((classes, CMP_DEV - 2, samples), binned.dtype)
-    x = jnp.concatenate([binned, right, middle, left], axis=1).astype(jnp.float32)
-    x = jnp.pad(x, ((0, 0), (0, 0), (0, 2 * LANES)))
     return panels(x, fold, offsets, velocities, samples)
 
 

time: 185 us -> 85.4 us (0.46)
  waiting for transfers between devices: 84.7 us -> 0 us
  Pallas kernels: 40.1 us -> 81.2 us
  starting transfers between devices: 31.9 us -> 0 us
  local copies, waits for them, and re-layouts: 22 us -> 2.63 us
  other arithmetic: 3.8 us -> 0.74 us
    all_to_all x4 -> x0, waiting for transfers between devices: 81.9 us -> none  [the longest x2 53.1 us: exchange(): lax.all_to_all(block, 'xline', split_axis=1, concat_axis=1, tiled=True)]
    pallas_call x0 -> x1, Pallas kernels: none -> 57.9 us  [gather(): pl.pallas_call(functools.partial(gather_kernel, dims), out_shape=(jax.Sha...]
    all_to_all x4 -> x0, starting transfers between devices: 26.6 us -> none  [the longest x2 14.9 us: exchange(): lax.all_to_all(block, 'inline', split_axis=0, concat_axis=0, tiled=True)]
    pallas_call x1, Pallas kernels: 40.1 us -> 23.2 us  [panels(): pl.pallas_call(panels_kernel, out_shape=(jax.ShapeDtypeStruct((mids, vels...]
    all_to_all x4 -> x0, local copies, waits for them, and re-layouts: 7.57 us -> none  [the longest x2 3.81 us: exchange(): lax.all_to_all(block, 'inline', split_axis=0, concat_axis=0, tiled=True)]
    reshape x5 -> x0, local copies, waits for them, and re-layouts: 6.5 us -> none  [the longest x1 2.74 us: per_device(): arrived = exchange(buffer).reshape(-1, samples)]
    ppermute x2 -> x0, starting transfers between devices: 5.28 us -> none  [the longest x1 3.36 us: per_device(): left = lax.ppermute(binned[:, CMP_DEV - 1:], axes, forward)]
    scatter x2 -> x0, local copies, waits for them, and re-layouts: 4.9 us -> none  [the longest x1 3.5 us: per_device(): jnp.zeros((devices * capacity, samples), traces.dtype).at[slot_row]]
  transfers between devices with their start and end apart: 6 -> 0, of which waited for: 5 -> 0; matrix products, arithmetic and copies ran while one was open for 7% -> 0% of each run, Pallas kernels for 0% -> 0%
where the time goes in v2:
time: 85.4 us; the launch traced here: 85.2 us
  Pallas kernels  81.2 us (95%)
  local copies, waits for them, and re-layouts  2.63 us (3%)
    pallas_call x1, Pallas kernels, gather(): pl.pallas_call(functools.partial(gather_kernel, dims), out_shape=(jax.Sha...  57.9 us
    pallas_call x1, Pallas kernels, panels(): pl.pallas_call(panels_kernel, out_shape=(jax.ShapeDtypeStruct((mids, vels...  23.2 us

profile of v2, /device:TPU:1, one launch (start us, length us, event | category | flops | bytes accessed | tf_op | source)
XLA Modules:
  0.0 85.2 jit_solution(12710514264202722346)
XLA Ops:
  0.6 0.0 copy-start.1
  0.6 0.0 copy-start
  0.7 0.6 copy-done.1
  1.3 0.0 copy-done
  1.3 0.6 multiply_add_fusion
  1.9 0.0 copy-start.2
  1.9 0.0 copy-start.3
  1.9 0.7 copy-done.2
  2.5 0.0 copy-done.3
  2.6 0.1 divide_multiply_fusion
  2.6 0.6 mul.34.slow_ref
  3.3 0.1 minimum_convert_fusion
  3.4 0.7 reshape.59.start_ref
  4.0 57.9 %gather.1 = (f32[4,16,2304]{2,1,0:T(8,128)}, f32[8,128]{1,0:T(8,128)}) custom-call(bf16[256,2048]{1,0:T(8,128)(2,1)} %traces_ref.1, s32[1,256]{1,0:T(1,128)} %bitcast.3, s32[1,256]{1,0:T(1,128)} %bitcast.2), custom_call_target="tpu_custom_call" | custom-call | tf_op jit(solution)/shard_map/gather/pallas_call | solution.py:420
  62.0 23.2 %panels.1 = (bf16[8,16,2048]{2,1,0:T(8,128)(2,1)}, f32[8,16,2048]{2,1,0:T(8,128)}) custom-call(s32[1024]{0:T(1024)} %reshape.59.start_ref, f32[64]{0:T(128)} %mul.34.slow_ref, f32[4,16,2304]{2,1,0:T(8,128)} %get-tuple-element.4.x_ref, f32[8,128]{1,0:T(8,128)} %get-tuple-element.5.fold_ref), custom_call_target="tpu_custom_call" | custom-call | tf_op jit(solution)/shard_map/panels/pallas_call | solution.py:152
  (1 shorter events, 0.0 us)
Async XLA Ops:
  0.6 0.7 copy-start.1
  0.6 0.7 copy-start
  1.9 0.7 copy-start.2
  1.9 0.7 copy-start.3

commit v3 on v1

v3 whole, which is shorter than its diff:
```python
import functools

import jax
import jax.numpy as jnp
from jax import lax
from jax.experimental import pallas as pl
from jax.experimental.pallas import tpu as pltpu
from jax.sharding import PartitionSpec as P

CMP_DEV = 8
LANES = 128
GROUP = 8
MESH = pl.DeviceIdType.MESH


def take_lanes(values, index):
    return lax.gather(
        values, index[:, :, None],
        lax.GatherDimensionNumbers(
            offset_dims=(), collapsed_slice_dims=(1,), start_index_map=(1,),
            operand_batching_dims=(0,), start_indices_batching_dims=(0,)),
        slice_sizes=(1, 1), mode=lax.GatherScatterMode.PROMISE_IN_BOUNDS)


def log2(n):
    assert n & (n - 1) == 0
    return n.bit_length() - 1


def chunks_of(blocks):
    sizes = [2] * ((blocks - 2) // 2) + [1, 1]
    out, top = [], blocks
    for size in sizes:
        top -= size
        out.append((top, size))
    return out


def kernel(
    dims, traces_hbm, owner_ref, midpoint_ref, class_ref, offsets_ref, velocities_ref, start_s, start_v,
    stacked_ref, semblance_ref,
    traces, buf, arr, kout, karr, member, zout, zarr, cout, carr, eout, earr,
    xa, xb, at, low, high, power, energy, sums, ratio,
    plane_send, plane_recv, zed_send, zed_recv, rim_send, rim_recv, own_sem,
):
    nx, ny, nz = dims
    inline = nx * ny * 2
    rows, samples = traces.shape
    slots = buf.shape[0] // inline
    bins = zout.shape[1]
    mids, vels = semblance_ref.shape[:2]
    classes = bins // mids
    blocks = samples // LANES
    plan = chunks_of(blocks)
    last = len(plan)
    me, mz = lax.axis_index("inline"), lax.axis_index("xline")
    mx, my, mc = me >> (log2(ny) + 1), (me >> 1) & (ny - 1), me & 1

    def plane_peer(p):
        q = p >> 1
        tx, ty = q & (nx - 1), q >> log2(nx)
        dx = (nx // 2) ^ tx ^ (tx >> 1)
        dy = (ny // 2) ^ ty ^ (ty >> 1)
        px, py = (mx + dx) & (nx - 1), (my + dy) & (ny - 1)
        return (((px << log2(ny)) | py) << 1) | ((mc + 1 + p) & 1)

    def zed_peer(p):
        step = (p + 1) >> 1
        return (mz + jnp.where((p & 1) == 1, step, nz - step)) & (nz - 1)

    right = ((me + jnp.where(mz == nz - 1, 1, 0)) & (inline - 1), (mz + 1) & (nz - 1))
    left = ((me + jnp.where(mz == 0, inline - 1, 0)) & (inline - 1), (mz + nz - 1) & (nz - 1))

    barrier = pltpu.get_barrier_semaphore()

    def greet_plane(p, _):
        pl.semaphore_signal(barrier, inc=1, device_id=(plane_peer(p), mz), device_id_type=MESH)
        return 0

    def greet_zed(p, _):
        pl.semaphore_signal(barrier, inc=1, device_id=(me, zed_peer(p)), device_id_type=MESH)
        return 0

    traces_in = pltpu.make_async_copy(traces_hbm, traces, own_sem.at[0])
    traces_in.start()
    lax.fori_loop(1, nz, greet_zed, 0)
    lax.fori_loop(0, inline - 1, greet_plane, 0)
    for peer in (left, right):
        pl.semaphore_signal(barrier, inc=1, device_id=peer, device_id_type=MESH)

    square = (rows, rows)
    first = lax.broadcasted_iota(jnp.int32, square, 0)
    second = lax.broadcasted_iota(jnp.int32, square, 1)
    owner_row = owner_ref[...]
    owner_all = jnp.broadcast_to(owner_row.astype(jnp.float32), square)
    owner_col = jnp.sum(jnp.where(first == second, owner_all, 0.0), axis=1, keepdims=True)
    same = owner_all == owner_col
    rank_row = jnp.sum(jnp.where(same & (first < second), 1.0, 0.0), axis=0, keepdims=True).astype(jnp.int32)
    rank_col = jnp.sum(jnp.where(same & (second < first), 1.0, 0.0), axis=1, keepdims=True).astype(jnp.int32)
    capacity = slots // nz
    slot_row = owner_row * capacity + rank_row
    wide = (inline * slots, rows)
    member[0:inline * slots, 0:rows] = jnp.where(
        lax.broadcasted_iota(jnp.int32, wide, 0) == slot_row, 1.0, 0.0).astype(jnp.bfloat16)
    per_lane = 128 // slots
    owner_col = owner_col.astype(jnp.int32)
    lane_at = (me & (per_lane - 1)) * slots + (owner_col & (nz - 1)) * capacity + rank_col
    placed = jnp.where(
        lax.broadcasted_iota(jnp.int32, (rows, 128), 1) == lane_at, 1.0, 0.0).astype(jnp.bfloat16)
    key = class_ref[...] * mids + midpoint_ref[...]
    number = ((owner_row & (nz - 1)) * bins + key + 1).astype(jnp.float32)
    chosen = jnp.where(
        lax.broadcasted_iota(jnp.int32, (inline, rows), 0) == owner_row >> log2(nz), number, 0.0
    ).astype(jnp.bfloat16)
    keys = jnp.dot(chosen, placed, preferred_element_type=jnp.float32)
    for i in range(inline):
        kout[i] = keys[i:i + 1, :]

    def cut(c):
        return pl.ds(plan[c][0] * LANES, plan[c][1] * LANES)

    def place(c):
        buf[:, cut(c)] = jnp.dot(
            member[0:inline * slots, 0:rows], traces[:, cut(c)],
            preferred_element_type=jnp.float32).astype(jnp.bfloat16)

    traces_in.wait()
    place(0)
    place(1)

    def prepare(g, _):
        row = lax.broadcasted_iota(jnp.int32, (blocks, LANES), 0)
        lane = lax.broadcasted_iota(jnp.int32, (blocks, LANES), 1)
        time = (row * LANES + lane).astype(jnp.float32)
        diagonal = lax.broadcasted_iota(jnp.int32, (blocks, blocks), 0) == lax.broadcasted_iota(
            jnp.int32, (blocks, blocks), 1)
        speed = jnp.full((1, LANES), velocities_ref[g])
        for h in range(classes):
            slowness = jnp.full((1, LANES), offsets_ref[h]) / speed
            slow = slowness * slowness
            position = jnp.sqrt(time * time + slow)
            starts = jnp.broadcast_to(
                start_v[pl.ds(g * classes + h, 1), :].astype(jnp.float32), (blocks, blocks))
            starts = jnp.sum(jnp.where(diagonal, starts, 0.0), axis=1, keepdims=True)
            floored = jnp.minimum(jnp.floor(position), float(samples))
            floored = jnp.minimum(jnp.maximum(floored, starts), starts + (LANES - 1))
            fraction = position - floored
            index = floored.astype(jnp.int32)
            here = pl.ds(pl.multiple_of((g * classes + h) * blocks, blocks), blocks)
            at[here, :] = index & (LANES - 1)
            low[here, :] = (1.0 - fraction).astype(jnp.bfloat16).astype(jnp.float32)
            high[here, :] = fraction.astype(jnp.bfloat16).astype(jnp.float32)
        return 0

    lax.fori_loop(0, vels, prepare, 0)

    pl.semaphore_wait(barrier, inline - 1 + nz - 1 + 2)

    own = pl.ds(pl.multiple_of(me * slots, slots), slots)

    def send_plane(c):
        def send(p, _):
            peer = plane_peer(p)
            pltpu.make_async_remote_copy(
                src_ref=buf.at[pl.ds(pl.multiple_of(peer * slots, slots), slots), cut(c)],
                dst_ref=arr.at[own, cut(c)],
                send_sem=plane_send.at[c], recv_sem=plane_recv.at[c],
                device_id=(peer, mz), device_id_type=MESH).start()
            return 0
        lax.fori_loop(0, inline - 1, send, 0)

    def send_key(p, _):
        peer = plane_peer(p)
        pltpu.make_async_remote_copy(
            src_ref=kout.at[peer], dst_ref=karr.at[me],
            send_sem=plane_send.at[last], recv_sem=plane_recv.at[last],
            device_id=(peer, mz), device_id_type=MESH).start()
        return 0

    send_plane(0)
    lax.fori_loop(0, inline - 1, send_key, 0)
    send_plane(1)
    for c in range(2, last):
        place(c)
        send_plane(c)
    own_copy = pltpu.make_async_copy(buf.at[own, :], arr.at[own, :], own_sem.at[1])
    own_copy.start()

    for plane in (power, energy):
        plane[:, 0:LANES] = jnp.zeros((vels * mids, LANES), jnp.float32)
        plane[:, LANES + samples:] = jnp.zeros((vels * mids, LANES), jnp.float32)
    for x in (xa, xb):
        for h in range(classes):
            x[h, :, samples:] = jnp.zeros((2 * mids, 2 * LANES), jnp.float32)

    def all_of(ref, sem):
        pltpu.make_async_copy(ref, ref, sem).wait()

    karr[me] = kout[me]
    all_of(karr.at[pl.ds(0, inline - 1)], plane_recv.at[last])
    arrived = inline * slots
    for q in range(inline // per_lane):
        line = karr[q * per_lane]
        for s in range(1, per_lane):
            line = line + karr[q * per_lane + s]
        number_at = lax.broadcasted_iota(jnp.int32, (nz * bins, 128), 0) + 1
        member[0:nz * bins, q * 128:(q + 1) * 128] = jnp.where(
            line.astype(jnp.int32) == number_at, 1.0, 0.0).astype(jnp.bfloat16)
    counts = jnp.dot(
        member[0:nz * bins, 0:arrived], jnp.ones((arrived, 128), jnp.bfloat16),
        preferred_element_type=jnp.float32)
    for z in range(nz):
        cout[z] = counts[z * bins:(z + 1) * bins]
    carr[mz] = cout[mz]
    own_copy.wait()

    def send_count(p, _):
        peer = zed_peer(p)
        pltpu.make_async_remote_copy(
            src_ref=cout.at[peer], dst_ref=carr.at[mz],
            send_sem=zed_send.at[last], recv_sem=zed_recv.at[last],
            device_id=(me, peer), device_id_type=MESH).start()
        return 0

    def bin_chunk(c):
        all_of(arr.at[pl.ds(0, (inline - 1) * slots), cut(c)], plane_recv.at[c])
        part = jnp.dot(
            member[0:nz * bins, 0:arrived], arr[:, cut(c)],
            preferred_element_type=jnp.float32).astype(jnp.bfloat16)
        for z in range(nz):
            zout[z, :, cut(c)] = part[z * bins:(z + 1) * bins]

        def send(p, _):
            peer = zed_peer(p)
            pltpu.make_async_remote_copy(
                src_ref=zout.at[peer, :, cut(c)], dst_ref=zarr.at[mz, :, cut(c)],
                send_sem=zed_send.at[c], recv_sem=zed_recv.at[c],
                device_id=(me, peer), device_id_type=MESH).start()
            return 0

        lax.fori_loop(1, nz, send, 0)
        if c == 0:
            lax.fori_loop(1, nz, send_count, 0)
        zarr[mz, :, cut(c)] = zout[mz, :, cut(c)]

    def rim_copies(c):
        return [pltpu.make_async_remote_copy(
            src_ref=eout.at[side, :, cut(c)], dst_ref=earr.at[side, :, cut(c)],
            send_sem=rim_send.at[side, c], recv_sem=rim_recv.at[side, c],
            device_id=peer, device_id_type=MESH) for side, peer in ((0, left), (1, right))]

    shape = (mids, LANES)
    lane = lax.broadcasted_iota(jnp.int32, shape, 1)
    sub = lax.broadcasted_iota(jnp.int32, shape, 0)

    def keep(h, at_row, b, part):
        here = pl.ds(b * LANES, LANES)
        xa[h, at_row:at_row + mids, here] = part
        after = xa[h, at_row:at_row + mids, (b + 1) * LANES:(b + 2) * LANES]
        xb[h, at_row:at_row + mids, here] = jnp.where(
            lane < LANES - 1, pltpu.roll(part, LANES - 1, 1), pltpu.roll(after, LANES - 1, 1))

    def sum_chunk(c):
        all_of(zarr.at[pl.ds(0, nz - 1), :, cut(c)], zed_recv.at[c])
        begin, count = plan[c]
        for b in reversed(range(begin, begin + count)):
            here = pl.ds(b * LANES, LANES)
            total = zarr[0, :, here].astype(jnp.float32)
            for z in range(1, nz):
                total = total + zarr[z, :, here].astype(jnp.float32)
            total = total.astype(jnp.bfloat16).astype(jnp.float32)
            for h in range(classes):
                part = total[h * mids:(h + 1) * mids]
                eout[0, h:h + 1, here] = part[0:1]
                eout[1, h:h + 1, here] = part[mids - 1:mids]
                keep(h, 0, b, part)
        for copy in rim_copies(c):
            copy.start()

    is_first = (me == 0) & (mz == 0)
    is_last = (me == inline - 1) & (mz == nz - 1)
    take_right = jnp.where(is_last, 0.0, jnp.where(sub == 0, 1.0, 0.0))
    take_left = jnp.where(is_first, 0.0, jnp.where(sub == mids - 1, 1.0, 0.0))

    def rim_chunk(c):
        for copy in rim_copies(c):
            copy.wait_recv()
        begin, count = plan[c]
        for b in reversed(range(begin, begin + count)):
            here = pl.ds(b * LANES, LANES)
            for h in range(classes):
                keep(h, mids, b, take_right * earr[0, h:h + 1, here] + take_left * earr[1, h:h + 1, here])

    def three(mine, rim):
        up = pltpu.roll(jnp.where(sub == mids - 1, rim, mine), 1, 0)
        down = pltpu.roll(jnp.where(sub == 0, rim, mine), mids - 1, 0)
        return mine + up + down

    def stack_one(g, b, scale):
        total = square_sum = rim_total = rim_square = jnp.zeros(shape, jnp.float32)
        for h in range(classes):
            pair = g * classes + h
            row = pl.ds(pair * blocks + b, 1)
            start = start_s[pair, b]
            near = pl.ds((start >> 7) * LANES, LANES)
            far = pl.ds((start >> 7) * LANES + LANES, LANES)
            mask = lane >= (start & (LANES - 1))
            index = jnp.broadcast_to(at[row, :], shape)
            weight_low = jnp.broadcast_to(low[row, :], shape)
            weight_high = jnp.broadcast_to(high[row, :], shape)
            moved = []
            for top in (0, mids):
                this = jnp.where(mask, xa[h, top:top + mids, near], xa[h, top:top + mids, far])
                after = jnp.where(mask, xb[h, top:top + mids, near], xb[h, top:top + mids, far])
                moved.append(weight_low * take_lanes(this, index) + weight_high * take_lanes(after, index))
            total += moved[0]
            square_sum += moved[0] * moved[0]
            rim_total += moved[1]
            rim_square += moved[1] * moved[1]
        here = pl.ds(pl.multiple_of(g * mids, mids), mids)
        sums[b, here, :] = total * scale
        power[here, (b + 1) * LANES:(b + 2) * LANES] = three(total * total, rim_total * rim_total)
        energy[here, (b + 1) * LANES:(b + 2) * LANES] = three(square_sum, rim_square)

    def stack_chunk(c, scale):
        begin, count = plan[c]
        step = 4 // count

        def some(i, _):
            for k in range(step):
                for b in range(begin, begin + count):
                    stack_one(i * step + k, b, scale)
            return 0

        lax.fori_loop(0, vels // step, some, 0)

    def finish(begin, end):
        width = (end - begin + 2) * LANES

        def window(plane, here):
            value = plane[here, begin * LANES:begin * LANES + width]
            by3 = value + pltpu.roll(value, 1, 1) + pltpu.roll(value, width - 1, 1)
            by9 = by3 + pltpu.roll(by3, 3, 1) + pltpu.roll(by3, width - 3, 1)
            return by9[:, LANES:width - LANES]

        def some(i, _):
            for k in range(4):
                here = pl.ds(pl.multiple_of((i * 4 + k) * mids, mids), mids)
                value = window(power, here) / jnp.maximum(classes * window(energy, here), 1.0)
                for b in range(begin, end):
                    ratio[b, here, :] = value[:, (b - begin) * LANES:(b - begin + 1) * LANES]
            return 0

        lax.fori_loop(0, vels // 4, some, 0)
        for b in range(begin, end):
            here = pl.ds(b * LANES, LANES)
            for m in range(mids):
                for half in range(vels // GROUP):
                    semblance_ref[m, half * GROUP:(half + 1) * GROUP, here] = ratio[
                        b, pl.ds(half * GROUP * mids + m, GROUP, stride=mids), :]
                stacked_ref[m, :, here] = jnp.concatenate([
                    sums[b, pl.ds(half * GROUP * mids + m, GROUP, stride=mids), :]
                    for half in range(vels // GROUP)
                ], axis=0).astype(jnp.bfloat16)

    scale = None
    done = blocks
    for c in range(last + 2):
        if c < last:
            bin_chunk(c)
        if 1 <= c <= last:
            sum_chunk(c - 1)
        if c >= 2:
            if scale is None:
                all_of(carr.at[pl.ds(0, nz - 1)], zed_recv.at[last])
                total = carr[0]
                for z in range(1, nz):
                    total = total + carr[z]
                fold = total[0:mids]
                for h in range(1, classes):
                    fold = fold + total[h * mids:(h + 1) * mids]
                scale = 1.0 / jnp.maximum(fold, 1.0)
            rim_chunk(c - 2)
            stack_chunk(c - 2, scale)
            begin = plan[c - 2][0]
            ready = begin + 1 if begin else 0
            if ready < done:
                finish(ready, done)
                done = ready

    for c in range(last):
        for copy in rim_copies(c):
            copy.wait_send()
        all_of(buf.at[pl.ds(0, (inline - 1) * slots), cut(c)], plane_send.at[c])
        all_of(zout.at[pl.ds(0, nz - 1), :, cut(c)], zed_send.at[c])
    all_of(kout.at[pl.ds(0, inline - 1)], plane_send.at[last])
    all_of(cout.at[pl.ds(0, nz - 1)], zed_send.at[last])


def survey(dims, traces, owners, midpoint, offset_class, offsets, velocities, mids):
    nx, ny, nz = dims
    inline = nx * ny * 2
    rows, samples = traces.shape
    classes, vels = offsets.shape[0], velocities.shape[0]
    capacity = max(2, 2 * rows // (inline * nz))
    slots = nz * capacity
    bins = classes * mids
    blocks = samples // LANES
    last = len(chunks_of(blocks))
    f32, bf16, i32 = jnp.float32, jnp.bfloat16, jnp.int32
    smem = pl.BlockSpec(memory_space=pltpu.SMEM)
    vmem = pl.BlockSpec(memory_space=pltpu.VMEM)
    dma = pltpu.SemaphoreType.DMA
    pairs = vels * classes
    padded = samples + 2 * LANES
    slowness = offsets[None, :] / velocities[:, None]
    time = (jnp.arange(blocks) * LANES).astype(f32)
    position = jnp.sqrt(time * time + (slowness * slowness)[:, :, None])
    start = jnp.minimum(jnp.floor(position), float(samples)).astype(i32).reshape(pairs, blocks)
    return pl.pallas_call(
        functools.partial(kernel, dims),
        out_shape=(
            jax.ShapeDtypeStruct((mids, vels, samples), bf16),
            jax.ShapeDtypeStruct((mids, vels, samples), f32),
        ),
        in_specs=[pl.BlockSpec(memory_space=pl.ANY), vmem, vmem, vmem, smem, smem, smem, vmem],
        out_specs=(vmem, vmem),
        scratch_shapes=[
            pltpu.VMEM((rows, samples), bf16),
            pltpu.VMEM((inline * slots, samples), bf16),
            pltpu.VMEM((inline * slots, samples), bf16),
            pltpu.VMEM((inline, 1, 128), f32),
            pltpu.VMEM((inline, 1, 128), f32),
            pltpu.VMEM((max(inline * slots, nz * bins), max(rows, inline * slots)), bf16),
            pltpu.VMEM((nz, bins, samples), bf16),
            pltpu.VMEM((nz, bins, samples), bf16),
            pltpu.VMEM((nz, bins, 128), f32),
            pltpu.VMEM((nz, bins, 128), f32),
            pltpu.VMEM((2, classes, samples), f32),
            pltpu.VMEM((2, classes, samples), f32),
            pltpu.VMEM((classes, 2 * mids, padded), f32),
            pltpu.VMEM((classes, 2 * mids, padded), f32),
            pltpu.VMEM((pairs * blocks, LANES), i32),
            pltpu.VMEM((pairs * blocks, LANES), f32),
            pltpu.VMEM((pairs * blocks, LANES), f32),
            pltpu.VMEM((vels * mids, padded), f32),
            pltpu.VMEM((vels * mids, padded), f32),
            pltpu.VMEM((blocks, vels * mids, LANES), f32),
            pltpu.VMEM((blocks, vels * mids, LANES), f32),
            dma((last + 1,)), dma((last + 1,)),
            dma((last + 1,)), dma((last + 1,)),
            dma((2, last)), dma((2, last)), dma((2,)),
        ],
        compiler_params=pltpu.CompilerParams(collective_id=0, has_side_effects=True),
        name="survey",
    )(traces, owners, midpoint, offset_class, offsets, velocities, start, start)


def per_device(traces, owners, midpoint, offset_class, offsets, velocities):
    side = round((lax.axis_size("inline") // 2) ** 0.5)
    rows = traces.shape[0]
    return survey(
        (side, side, lax.axis_size("xline")), traces, owners.reshape(1, rows),
        midpoint.reshape(1, rows), offset_class.reshape(1, rows), offsets, velocities, CMP_DEV
    )


def solution(mesh):
    in_specs = (
        P(("inline", "xline"), None),
        P(("inline", "xline"), None),
        P(("inline", "xline")),
        P(("inline", "xline")),
        P(),
        P(),
    )
    out_specs = (P(("inline", "xline"), None, None), P(("inline", "xline"), None, None))
    return jax.shard_map(
        per_device, mesh=mesh, in_specs=in_specs, out_specs=out_specs, check_vma=False
    )
```

time: 185 us -> 77.2 us (0.42)
  waiting for transfers between devices: 84.7 us -> 0 us
  starting transfers between devices: 31.9 us -> 0 us
  Pallas kernels: 40.1 us -> 71.1 us
  local copies, waits for them, and re-layouts: 22 us -> 4.39 us
  other arithmetic: 3.8 us -> 0.72 us
    all_to_all x4 -> x0, waiting for transfers between devices: 81.9 us -> none  [the longest x2 53.1 us: exchange(): lax.all_to_all(block, 'xline', split_axis=1, concat_axis=1, tiled=True)]
    pallas_call x1, Pallas kernels: 40.1 us -> 71.1 us  [survey(): pl.pallas_call(functools.partial(kernel, dims), out_shape=(jax.ShapeDtype...]
    all_to_all x4 -> x0, starting transfers between devices: 26.6 us -> none  [the longest x2 14.9 us: exchange(): lax.all_to_all(block, 'inline', split_axis=0, concat_axis=0, tiled=True)]
    all_to_all x4 -> x0, local copies, waits for them, and re-layouts: 7.57 us -> none  [the longest x2 3.81 us: exchange(): lax.all_to_all(block, 'inline', split_axis=0, concat_axis=0, tiled=True)]
    reshape x5 -> x0, local copies, waits for them, and re-layouts: 6.5 us -> none  [the longest x1 2.74 us: per_device(): arrived = exchange(buffer).reshape(-1, samples)]
    ppermute x2 -> x0, starting transfers between devices: 5.28 us -> none  [the longest x1 3.36 us: per_device(): left = lax.ppermute(binned[:, CMP_DEV - 1:], axes, forward)]
    scatter x2 -> x0, local copies, waits for them, and re-layouts: 4.9 us -> none  [the longest x1 3.5 us: per_device(): jnp.zeros((devices * capacity, samples), traces.dtype).at[slot_row]]
    unnamed x5 -> x8, local copies, waits for them, and re-layouts: 0.01 us -> 4.15 us
  transfers between devices with their start and end apart: 6 -> 0, of which waited for: 5 -> 0; matrix products, arithmetic and copies ran while one was open for 7% -> 0% of each run, Pallas kernels for 0% -> 0%
where the time goes in v3:
time: 77.2 us; the launch traced here: 76.9 us
  Pallas kernels  71.1 us (92%)
  local copies, waits for them, and re-layouts  4.39 us (6%)
    pallas_call x1, Pallas kernels, survey(): pl.pallas_call(functools.partial(kernel, dims), out_shape=(jax.ShapeDtype...  71.1 us
    unnamed x8, local copies, waits for them, and re-layouts  4.15 us

profile of v3, /device:TPU:1, one launch (start us, length us, event | category | flops | bytes accessed | tf_op | source)
XLA Modules:
  0.0 76.9 jit_solution(10485678585876570660)
XLA Ops:
  0.6 0.0 copy-start.1
  0.7 0.6 copy-done.1
  1.3 0.0 copy-start.2
  1.3 0.1 div.22
  1.4 0.6 copy-done.2
  1.9 0.1 div.23
  2.0 0.1 div.24
  2.1 0.7 minimum_convert_fusion.start_s.start_v
  2.8 71.1 %survey.1 = (bf16[8,16,2048]{2,1,0:T(8,128)(2,1)}, f32[8,16,2048]{2,1,0:T(8,128)}) custom-call(bf16[256,2048]{1,0:T(8,128)(2,1)} %traces_hbm.1, s32[1,256]{1,0:T(1,128)} %bitcast.5, s32[1,256]{1,0:T(1,128)} %bitcast.6, s32[1,256]{1,0:T(1,128)} %bitcast.7, f32[4]{0:T(128)} %offsets_ref.1, f32[16]{0:T(128)} %velocities_ref.1, ...), custom_call_target="tpu_custom_call" | custom-call | tf_op jit(solution)/shard_map/survey/pallas_call | solution.py:420
  74.0 0.0 copy-start
  74.0 2.0 %copy.11 = bf16[8,16,2048]{2,1,0:T(8,128)(2,1)} copy(bf16[8,16,2048]{2,1,0:T(8,128)(2,1)} %get-tuple-element.4) | data formatting | bytes 1048576
  76.0 0.0 copy-done
  76.0 1.0 %copy.12 = f32[8,16,2048]{2,1,0:T(8,128)} copy(f32[8,16,2048]{2,1,0:T(8,128)S(1)} %copy-done) | data formatting | bytes 2097152
  (3 shorter events, 0.0 us)
Async XLA Ops:
  0.6 0.7 copy-start.1
  1.3 0.7 copy-start.2
  74.0 2.0 %copy-start = (f32[8,16,2048]{2,1,0:T(8,128)S(1)}, f32[8,16,2048]{2,1,0:T(8,128)}, u32[]{:S(2)}) copy-start(f32[8,16,2048]{2,1,0:T(8,128)} %get-tuple-element.5) | copy-start | bytes 3145732

commit v4 on v3

--- a/solution.py
+++ b/solution.py
@@ -10,6 +10,7 @@
 CMP_DEV = 8
 LANES = 128
 GROUP = 8
+AHEAD = 3
 MESH = pl.DeviceIdType.MESH
 
 
@@ -28,7 +29,8 @@
 
 
 def chunks_of(blocks):
-    sizes = [2] * ((blocks - 2) // 2) + [1, 1]
+    sizes = [3] * ((blocks - 4) // 3) + [2, 1, 1]
+    assert sum(sizes) == blocks
     out, top = [], blocks
     for size in sizes:
         top -= size
@@ -39,8 +41,8 @@
 def kernel(
     dims, traces_hbm, owner_ref, midpoint_ref, class_ref, offsets_ref, velocities_ref, start_s, start_v,
     stacked_ref, semblance_ref,
-    traces, buf, arr, kout, karr, member, zout, zarr, cout, carr, eout, earr,
-    xa, xb, at, low, high, power, energy, sums, ratio,
+    traces, buf, arr, kout, karr, outgoing, member, zout, zarr, cout, carr, eout, earr,
+    xs, above, at, low, high, power, energy, sums, ratio,
     plane_send, plane_recv, zed_send, zed_recv, rim_send, rim_recv, own_sem,
 ):
     nx, ny, nz = dims
@@ -81,7 +83,7 @@
         pl.semaphore_signal(barrier, inc=1, device_id=(me, zed_peer(p)), device_id_type=MESH)
         return 0
 
-    traces_in = pltpu.make_async_copy(traces_hbm, traces, own_sem.at[0])
+    traces_in = pltpu.make_async_copy(traces_hbm, traces, own_sem)
     traces_in.start()
     lax.fori_loop(1, nz, greet_zed, 0)
     lax.fori_loop(0, inline - 1, greet_plane, 0)
@@ -100,7 +102,7 @@
     capacity = slots // nz
     slot_row = owner_row * capacity + rank_row
     wide = (inline * slots, rows)
-    member[0:inline * slots, 0:rows] = jnp.where(
+    outgoing[...] = jnp.where(
         lax.broadcasted_iota(jnp.int32, wide, 0) == slot_row, 1.0, 0.0).astype(jnp.bfloat16)
     per_lane = 128 // slots
     owner_col = owner_col.astype(jnp.int32)
@@ -121,7 +123,7 @@
 
     def place(c):
         buf[:, cut(c)] = jnp.dot(
-            member[0:inline * slots, 0:rows], traces[:, cut(c)],
+            outgoing[...], traces[:, cut(c)],
             preferred_element_type=jnp.float32).astype(jnp.bfloat16)
 
     traces_in.wait()
@@ -180,18 +182,17 @@
     send_plane(0)
     lax.fori_loop(0, inline - 1, send_key, 0)
     send_plane(1)
-    for c in range(2, last):
+    for c in range(2, AHEAD):
         place(c)
         send_plane(c)
-    own_copy = pltpu.make_async_copy(buf.at[own, :], arr.at[own, :], own_sem.at[1])
-    own_copy.start()
 
     for plane in (power, energy):
         plane[:, 0:LANES] = jnp.zeros((vels * mids, LANES), jnp.float32)
         plane[:, LANES + samples:] = jnp.zeros((vels * mids, LANES), jnp.float32)
-    for x in (xa, xb):
-        for h in range(classes):
-            x[h, :, samples:] = jnp.zeros((2 * mids, 2 * LANES), jnp.float32)
+    for h in range(classes):
+        for kind in range(2):
+            xs[h, kind, :, samples:] = jnp.zeros((2 * mids, 2 * LANES), jnp.bfloat16)
+            above[h, kind] = jnp.zeros((mids, LANES), jnp.float32)
 
     def all_of(ref, sem):
         pltpu.make_async_copy(ref, ref, sem).wait()
@@ -204,15 +205,14 @@
         for s in range(1, per_lane):
             line = line + karr[q * per_lane + s]
         number_at = lax.broadcasted_iota(jnp.int32, (nz * bins, 128), 0) + 1
-        member[0:nz * bins, q * 128:(q + 1) * 128] = jnp.where(
+        member[:, q * 128:(q + 1) * 128] = jnp.where(
             line.astype(jnp.int32) == number_at, 1.0, 0.0).astype(jnp.bfloat16)
     counts = jnp.dot(
-        member[0:nz * bins, 0:arrived], jnp.ones((arrived, 128), jnp.bfloat16),
+        member[...], jnp.ones((arrived, 128), jnp.bfloat16),
         preferred_element_type=jnp.float32)
     for z in range(nz):
         cout[z] = counts[z * bins:(z + 1) * bins]
     carr[mz] = cout[mz]
-    own_copy.wait()
 
     def send_count(p, _):
         peer = zed_peer(p)
@@ -223,9 +223,10 @@
         return 0
 
     def bin_chunk(c):
+        arr[own, cut(c)] = buf[own, cut(c)]
         all_of(arr.at[pl.ds(0, (inline - 1) * slots), cut(c)], plane_recv.at[c])
         part = jnp.dot(
-            member[0:nz * bins, 0:arrived], arr[:, cut(c)],
+            member[...], arr[:, cut(c)],
             preferred_element_type=jnp.float32).astype(jnp.bfloat16)
         for z in range(nz):
             zout[z, :, cut(c)] = part[z * bins:(z + 1) * bins]
@@ -242,6 +243,9 @@
         if c == 0:
             lax.fori_loop(1, nz, send_count, 0)
         zarr[mz, :, cut(c)] = zout[mz, :, cut(c)]
+        if c + AHEAD < last:
+            place(c + AHEAD)
+            send_plane(c + AHEAD)
 
     def rim_copies(c):
         return [pltpu.make_async_remote_copy(
@@ -252,13 +256,14 @@
     shape = (mids, LANES)
     lane = lax.broadcasted_iota(jnp.int32, shape, 1)
     sub = lax.broadcasted_iota(jnp.int32, shape, 0)
-
-    def keep(h, at_row, b, part):
-        here = pl.ds(b * LANES, LANES)
-        xa[h, at_row:at_row + mids, here] = part
-        after = xa[h, at_row:at_row + mids, (b + 1) * LANES:(b + 2) * LANES]
-        xb[h, at_row:at_row + mids, here] = jnp.where(
-            lane < LANES - 1, pltpu.roll(part, LANES - 1, 1), pltpu.roll(after, LANES - 1, 1))
+    lane16 = lax.broadcasted_iota(jnp.int32, (2 * mids, LANES), 1).astype(jnp.int16)
+
+    def keep(h, kind, b, part):
+        shifted = jnp.where(
+            lane < LANES - 1, pltpu.roll(part, LANES - 1, 1), pltpu.roll(above[h, kind], LANES - 1, 1))
+        above[h, kind] = part
+        xs[h, kind, :, pl.ds(b * LANES, LANES)] = jnp.concatenate(
+            [part, shifted], axis=0).astype(jnp.bfloat16)
 
     def sum_chunk(c):
         all_of(zarr.at[pl.ds(0, nz - 1), :, cut(c)], zed_recv.at[c])
@@ -289,7 +294,7 @@
         for b in reversed(range(begin, begin + count)):
             here = pl.ds(b * LANES, LANES)
             for h in range(classes):
-                keep(h, mids, b, take_right * earr[0, h:h + 1, here] + take_left * earr[1, h:h + 1, here])
+                keep(h, 1, b, take_right * earr[0, h:h + 1, here] + take_left * earr[1, h:h + 1, here])
 
     def three(mine, rim):
         up = pltpu.roll(jnp.where(sub == mids - 1, rim, mine), 1, 0)
@@ -304,15 +309,16 @@
             start = start_s[pair, b]
             near = pl.ds((start >> 7) * LANES, LANES)
             far = pl.ds((start >> 7) * LANES + LANES, LANES)
-            mask = lane >= (start & (LANES - 1))
-            index = jnp.broadcast_to(at[row, :], shape)
+            mask = lane16 >= jnp.full((2 * mids, LANES), start & (LANES - 1), jnp.int32).astype(jnp.int16)
+            index = jnp.broadcast_to(at[row, :], (2 * mids, LANES)).astype(jnp.int16)
             weight_low = jnp.broadcast_to(low[row, :], shape)
             weight_high = jnp.broadcast_to(high[row, :], shape)
             moved = []
-            for top in (0, mids):
-                this = jnp.where(mask, xa[h, top:top + mids, near], xa[h, top:top + mids, far])
-                after = jnp.where(mask, xb[h, top:top + mids, near], xb[h, top:top + mids, far])
-                moved.append(weight_low * take_lanes(this, index) + weight_high * take_lanes(after, index))
+            for kind in range(2):
+                picked = take_lanes(
+                    jnp.where(mask, xs[h, kind, :, near], xs[h, kind, :, far]), index
+                ).astype(jnp.float32)
+                moved.append(weight_low * picked[0:mids] + weight_high * picked[mids:])
             total += moved[0]
             square_sum += moved[0] * moved[0]
             rim_total += moved[1]
@@ -324,7 +330,7 @@
 
     def stack_chunk(c, scale):
         begin, count = plan[c]
-        step = 4 // count
+        step = {1: 8, 2: 4}.get(count, 2)
 
         def some(i, _):
             for k in range(step):
@@ -431,15 +437,16 @@
             pltpu.VMEM((inline * slots, samples), bf16),
             pltpu.VMEM((inline, 1, 128), f32),
             pltpu.VMEM((inline, 1, 128), f32),
-            pltpu.VMEM((max(inline * slots, nz * bins), max(rows, inline * slots)), bf16),
+            pltpu.VMEM((inline * slots, rows), bf16),
+            pltpu.VMEM((nz * bins, inline * slots), bf16),
             pltpu.VMEM((nz, bins, samples), bf16),
             pltpu.VMEM((nz, bins, samples), bf16),
             pltpu.VMEM((nz, bins, 128), f32),
             pltpu.VMEM((nz, bins, 128), f32),
             pltpu.VMEM((2, classes, samples), f32),
             pltpu.VMEM((2, classes, samples), f32),
-            pltpu.VMEM((classes, 2 * mids, padded), f32),
-            pltpu.VMEM((classes, 2 * mids, padded), f32),
+            pltpu.VMEM((classes, 2, 2 * mids, padded), bf16),
+            pltpu.VMEM((classes, 2, mids, LANES), f32),
             pltpu.VMEM((pairs * blocks, LANES), i32),
             pltpu.VMEM((pairs * blocks, LANES), f32),
             pltpu.VMEM((pairs * blocks, LANES), f32),
@@ -449,7 +456,7 @@
             pltpu.VMEM((blocks, vels * mids, LANES), f32),
             dma((last + 1,)), dma((last + 1,)),
             dma((last + 1,)), dma((last + 1,)),
-            dma((2, last)), dma((2, last)), dma((2,)),
+            dma((2, last)), dma((2, last)), dma,
         ],
         compiler_params=pltpu.CompilerParams(collective_id=0, has_side_effects=True),
         name="survey",

time: 77.2 us -> 72.7 us (0.942)
  Pallas kernels: 71.1 us -> 66.6 us
    pallas_call x1, Pallas kernels: 71.1 us -> 66.6 us  [survey(): pl.pallas_call(functools.partial(kernel, dims), out_shape=(jax.ShapeDtype...]
where the time goes in v4:
time: 72.7 us; the launch traced here: 72.4 us
  Pallas kernels  66.6 us (92%)
  local copies, waits for them, and re-layouts  4.39 us (6%)
    pallas_call x1, Pallas kernels, survey(): pl.pallas_call(functools.partial(kernel, dims), out_shape=(jax.ShapeDtype...  66.6 us
    unnamed x8, local copies, waits for them, and re-layouts  4.15 us

profile of v4, /device:TPU:1, one launch (start us, length us, event | category | flops | bytes accessed | tf_op | source)
XLA Modules:
  0.0 72.4 jit_solution(13985699339986006719)
XLA Ops:
  0.6 0.0 copy-start.1
  0.7 0.6 copy-done.1
  1.3 0.0 copy-start.2
  1.3 0.1 div.22
  1.4 0.6 copy-done.2
  1.9 0.1 div.23
  2.0 0.1 div.24
  2.1 0.7 minimum_convert_fusion.start_s.start_v
  2.8 66.6 %survey.1 = (bf16[8,16,2048]{2,1,0:T(8,128)(2,1)}, f32[8,16,2048]{2,1,0:T(8,128)}) custom-call(bf16[256,2048]{1,0:T(8,128)(2,1)} %traces_hbm.1, s32[1,256]{1,0:T(1,128)} %bitcast.5, s32[1,256]{1,0:T(1,128)} %bitcast.6, s32[1,256]{1,0:T(1,128)} %bitcast.7, f32[4]{0:T(128)} %offsets_ref.1, f32[16]{0:T(128)} %velocities_ref.1, ...), custom_call_target="tpu_custom_call" | custom-call | tf_op jit(solution)/shard_map/survey/pallas_call | solution.py:426
  69.5 0.0 copy-start
  69.5 2.0 %copy.11 = bf16[8,16,2048]{2,1,0:T(8,128)(2,1)} copy(bf16[8,16,2048]{2,1,0:T(8,128)(2,1)} %get-tuple-element.4) | data formatting | bytes 1048576
  71.4 0.0 copy-done
  71.4 1.0 %copy.12 = f32[8,16,2048]{2,1,0:T(8,128)} copy(f32[8,16,2048]{2,1,0:T(8,128)S(1)} %copy-done) | data formatting | bytes 2097152
  (3 shorter events, 0.0 us)
Async XLA Ops:
  0.6 0.7 copy-start.1
  1.3 0.7 copy-start.2
  69.5 2.0 %copy-start = (f32[8,16,2048]{2,1,0:T(8,128)S(1)}, f32[8,16,2048]{2,1,0:T(8,128)}, u32[]{:S(2)}) copy-start(f32[8,16,2048]{2,1,0:T(8,128)} %get-tuple-element.5) | copy-start | bytes 3145732

commit v5 on v4

--- a/solution.py
+++ b/solution.py
@@ -10,7 +10,12 @@
 CMP_DEV = 8
 LANES = 128
 GROUP = 8
-AHEAD = 3
+HALF_WIN = 4
+AHEAD = 8
+VMEM_LIMIT = 24 << 20
+SUM_LAG = 2
+STACK_LAG = 4
+SIZES = (1, 2, 3, 3, 3, 2, 1, 1)
 MESH = pl.DeviceIdType.MESH
 
 
@@ -29,8 +34,7 @@
 
 
 def chunks_of(blocks):
-    sizes = [3] * ((blocks - 4) // 3) + [2, 1, 1]
-    assert sum(sizes) == blocks
+    sizes = SIZES if sum(SIZES) == blocks else [1] * blocks
     out, top = [], blocks
     for size in sizes:
         top -= size
@@ -42,7 +46,7 @@
     dims, traces_hbm, owner_ref, midpoint_ref, class_ref, offsets_ref, velocities_ref, start_s, start_v,
     stacked_ref, semblance_ref,
     traces, buf, arr, kout, karr, outgoing, member, zout, zarr, cout, carr, eout, earr,
-    xs, above, at, low, high, power, energy, sums, ratio,
+    xs, above, at, low, high, planes, band, sums, ratio,
     plane_send, plane_recv, zed_send, zed_recv, rim_send, rim_recv, own_sem,
 ):
     nx, ny, nz = dims
@@ -127,8 +131,8 @@
             preferred_element_type=jnp.float32).astype(jnp.bfloat16)
 
     traces_in.wait()
-    place(0)
-    place(1)
+    for c in range(last):
+        place(c)
 
     def prepare(g, _):
         row = lax.broadcasted_iota(jnp.int32, (blocks, LANES), 0)
@@ -156,9 +160,31 @@
 
     lax.fori_loop(0, vels, prepare, 0)
 
+    for k in range(4):
+        planes[k, :, 0:LANES] = jnp.zeros((vels * mids, LANES), jnp.bfloat16)
+        planes[k, :, LANES + samples:] = jnp.zeros((vels * mids, LANES), jnp.bfloat16)
+    band_shape = (3 * LANES, LANES)
+    away = lax.broadcasted_iota(jnp.int32, band_shape, 0) - LANES - lax.broadcasted_iota(
+        jnp.int32, band_shape, 1)
+    band[...] = jnp.where(
+        (away <= HALF_WIN) & (away >= -HALF_WIN), 1.0, 0.0).astype(jnp.bfloat16)
+    for h in range(classes):
+        for kind in range(2):
+            xs[h, kind, :, samples:] = jnp.zeros((2 * mids, 2 * LANES), jnp.bfloat16)
+            above[h, kind] = jnp.zeros((mids, LANES), jnp.float32)
+
     pl.semaphore_wait(barrier, inline - 1 + nz - 1 + 2)
 
     own = pl.ds(pl.multiple_of(me * slots, slots), slots)
+
+    def several(send):
+        def some(i, _):
+            for k in range(4):
+                send(i * 4 + k, 0)
+            return 0
+        lax.fori_loop(0, (inline - 1) // 4, some, 0)
+        for p in range((inline - 1) // 4 * 4, inline - 1):
+            send(p, 0)
 
     def send_plane(c):
         def send(p, _):
@@ -169,7 +195,7 @@
                 send_sem=plane_send.at[c], recv_sem=plane_recv.at[c],
                 device_id=(peer, mz), device_id_type=MESH).start()
             return 0
-        lax.fori_loop(0, inline - 1, send, 0)
+        several(send)
 
     def send_key(p, _):
         peer = plane_peer(p)
@@ -179,20 +205,10 @@
             device_id=(peer, mz), device_id_type=MESH).start()
         return 0
 
+    several(send_key)
     send_plane(0)
-    lax.fori_loop(0, inline - 1, send_key, 0)
-    send_plane(1)
-    for c in range(2, AHEAD):
-        place(c)
+    for c in range(1, min(AHEAD, last)):
         send_plane(c)
-
-    for plane in (power, energy):
-        plane[:, 0:LANES] = jnp.zeros((vels * mids, LANES), jnp.float32)
-        plane[:, LANES + samples:] = jnp.zeros((vels * mids, LANES), jnp.float32)
-    for h in range(classes):
-        for kind in range(2):
-            xs[h, kind, :, samples:] = jnp.zeros((2 * mids, 2 * LANES), jnp.bfloat16)
-            above[h, kind] = jnp.zeros((mids, LANES), jnp.float32)
 
     def all_of(ref, sem):
         pltpu.make_async_copy(ref, ref, sem).wait()
@@ -244,7 +260,6 @@
             lax.fori_loop(1, nz, send_count, 0)
         zarr[mz, :, cut(c)] = zout[mz, :, cut(c)]
         if c + AHEAD < last:
-            place(c + AHEAD)
             send_plane(c + AHEAD)
 
     def rim_copies(c):
@@ -325,39 +340,42 @@
             rim_square += moved[1] * moved[1]
         here = pl.ds(pl.multiple_of(g * mids, mids), mids)
         sums[b, here, :] = total * scale
-        power[here, (b + 1) * LANES:(b + 2) * LANES] = three(total * total, rim_total * rim_total)
-        energy[here, (b + 1) * LANES:(b + 2) * LANES] = three(square_sum, rim_square)
+        return three(total * total, rim_total * rim_total), three(square_sum, rim_square)
+
+    def split(k, pair, b, even, odd):
+        here = pl.ds(pl.multiple_of(pair * 2 * mids, 2 * mids), 2 * mids)
+        columns = pl.ds((b + 1) * LANES, LANES)
+        value = jnp.concatenate([even, odd], axis=0)
+        upper = value.astype(jnp.bfloat16)
+        planes[2 * k, here, columns] = upper
+        planes[2 * k + 1, here, columns] = (value - upper.astype(jnp.float32)).astype(jnp.bfloat16)
 
     def stack_chunk(c, scale):
         begin, count = plan[c]
         step = {1: 8, 2: 4}.get(count, 2)
 
         def some(i, _):
-            for k in range(step):
+            for k in range(step // 2):
+                pair = i * (step // 2) + k
                 for b in range(begin, begin + count):
-                    stack_one(i * step + k, b, scale)
+                    even = stack_one(pair * 2, b, scale)
+                    odd = stack_one(pair * 2 + 1, b, scale)
+                    split(0, pair, b, even[0], odd[0])
+                    split(1, pair, b, even[1], odd[1])
             return 0
 
         lax.fori_loop(0, vels // step, some, 0)
 
     def finish(begin, end):
-        width = (end - begin + 2) * LANES
-
-        def window(plane, here):
-            value = plane[here, begin * LANES:begin * LANES + width]
-            by3 = value + pltpu.roll(value, 1, 1) + pltpu.roll(value, width - 1, 1)
-            by9 = by3 + pltpu.roll(by3, 3, 1) + pltpu.roll(by3, width - 3, 1)
-            return by9[:, LANES:width - LANES]
-
-        def some(i, _):
-            for k in range(4):
-                here = pl.ds(pl.multiple_of((i * 4 + k) * mids, mids), mids)
-                value = window(power, here) / jnp.maximum(classes * window(energy, here), 1.0)
-                for b in range(begin, end):
-                    ratio[b, here, :] = value[:, (b - begin) * LANES:(b - begin + 1) * LANES]
-            return 0
-
-        lax.fori_loop(0, vels // 4, some, 0)
+        def window(k, b):
+            columns = pl.ds(b * LANES, 3 * LANES)
+            return jnp.dot(
+                planes[2 * k, :, columns], band[...], preferred_element_type=jnp.float32
+            ) + jnp.dot(
+                planes[2 * k + 1, :, columns], band[...], preferred_element_type=jnp.float32)
+
+        for b in range(begin, end):
+            ratio[b] = window(0, b) / jnp.maximum(classes * window(1, b), 1.0)
         for b in range(begin, end):
             here = pl.ds(b * LANES, LANES)
             for m in range(mids):
@@ -371,12 +389,12 @@
 
     scale = None
     done = blocks
-    for c in range(last + 2):
+    for c in range(last + STACK_LAG):
         if c < last:
             bin_chunk(c)
-        if 1 <= c <= last:
-            sum_chunk(c - 1)
-        if c >= 2:
+        if 0 <= c - SUM_LAG < last:
+            sum_chunk(c - SUM_LAG)
+        if c >= STACK_LAG:
             if scale is None:
                 all_of(carr.at[pl.ds(0, nz - 1)], zed_recv.at[last])
                 total = carr[0]
@@ -386,9 +404,9 @@
                 for h in range(1, classes):
                     fold = fold + total[h * mids:(h + 1) * mids]
                 scale = 1.0 / jnp.maximum(fold, 1.0)
-            rim_chunk(c - 2)
-            stack_chunk(c - 2, scale)
-            begin = plan[c - 2][0]
+            rim_chunk(c - STACK_LAG)
+            stack_chunk(c - STACK_LAG, scale)
+            begin = plan[c - STACK_LAG][0]
             ready = begin + 1 if begin else 0
             if ready < done:
                 finish(ready, done)
@@ -450,15 +468,15 @@
             pltpu.VMEM((pairs * blocks, LANES), i32),
             pltpu.VMEM((pairs * blocks, LANES), f32),
             pltpu.VMEM((pairs * blocks, LANES), f32),
-            pltpu.VMEM((vels * mids, padded), f32),
-            pltpu.VMEM((vels * mids, padded), f32),
+            pltpu.VMEM((4, vels * mids, padded), bf16),
+            pltpu.VMEM((3 * LANES, LANES), bf16),
             pltpu.VMEM((blocks, vels * mids, LANES), f32),
             pltpu.VMEM((blocks, vels * mids, LANES), f32),
             dma((last + 1,)), dma((last + 1,)),
             dma((last + 1,)), dma((last + 1,)),
             dma((2, last)), dma((2, last)), dma,
         ],
-        compiler_params=pltpu.CompilerParams(collective_id=0, has_side_effects=True),
+        compiler_params=pltpu.CompilerParams(collective_id=0, has_side_effects=True, vmem_limit_bytes=VMEM_LIMIT),
         name="survey",
     )(traces, owners, midpoint, offset_class, offsets, velocities, start, start)
 

time: 72.7 us -> 61.2 us (0.84)
  Pallas kernels: 66.6 us -> 55.1 us
    pallas_call x1, Pallas kernels: 66.6 us -> 55.1 us  [survey(): pl.pallas_call(functools.partial(kernel, dims), out_shape=(jax.ShapeDtype...]
    unnamed x8 -> x14, local copies, waits for them, and re-layouts: 4.15 us -> 4.79 us
where the time goes in v5:
time: 61.2 us; the launch traced here: 60.9 us
  Pallas kernels  55.1 us (90%)
  local copies, waits for them, and re-layouts  5.03 us (8%)
  between operations  0.7 us (1%)
    pallas_call x1, Pallas kernels, survey(): pl.pallas_call(functools.partial(kernel, dims), out_shape=(jax.ShapeDtype...  55.1 us
    unnamed x14, local copies, waits for them, and re-layouts  4.79 us

profile of v5, /device:TPU:1, one launch (start us, length us, event | category | flops | bytes accessed | tf_op | source)
XLA Modules:
  0.0 60.9 jit_solution(16622708660711551020)
XLA Ops:
  0.6 0.0 copy-start.1
  0.7 0.6 %copy-done.1 = f32[4]{0:T(128)S(1)} copy-done((f32[4]{0:T(128)S(1)}, f32[4]{0:T(128)}, u32[]{:S(2)}) %copy-start.1) | copy-done | bytes 40
  1.3 0.0 copy-start.2
  1.3 0.1 div.22
  1.4 0.6 copy-done.2
  1.9 0.1 div.23
  2.0 0.1 div.24
  2.1 0.0 copy-start.3
  2.1 0.0 copy-start.4
  2.1 0.0 copy-start.5
  2.2 0.1 minimum_convert_fusion.start_s.start_v
  2.2 0.6 copy-done.3
  2.8 0.0 copy-done.4
  2.8 0.0 copy-done.5
  2.8 0.0 copy-start
  2.8 1.2 %copy-done = bf16[256,2048]{1,0:T(8,128)(2,1)S(1)} copy-done((bf16[256,2048]{1,0:T(8,128)(2,1)S(1)}, bf16[256,2048]{1,0:T(8,128)(2,1)}, u32[]{:S(2)}) %copy-start) | copy-done | bytes 1048600
  4.1 55.1 %survey.1 = (bf16[8,16,2048]{2,1,0:T(8,128)(2,1)S(1)}, f32[8,16,2048]{2,1,0:T(8,128)S(1)}) custom-call(bf16[256,2048]{1,0:T(8,128)(2,1)S(1)} %copy-done, s32[1,256]{1,0:T(1,128)S(1)} %bitcast.5, s32[1,256]{1,0:T(1,128)S(1)} %bitcast.6, s32[1,256]{1,0:T(1,128)S(1)} %bitcast.7, f32[4]{0:T(128)S(1)} %copy-done.1, f32[16]{0:T(128)S(1)} %copy-done.2, ...), custom_call_target="tpu_custom_call" | custom-call | tf_op jit(solution)/shard_map/survey/pallas_call | solution.py:444
  59.1 0.8 %copy.11 = bf16[8,16,2048]{2,1,0:T(8,128)(2,1)} copy(bf16[8,16,2048]{2,1,0:T(8,128)(2,1)S(1)} %get-tuple-element.4) | data formatting | bytes 1048576
  59.9 1.0 %copy.12 = f32[8,16,2048]{2,1,0:T(8,128)} copy(f32[8,16,2048]{2,1,0:T(8,128)S(1)} %get-tuple-element.5) | data formatting | bytes 2097152
  (3 shorter events, 0.0 us)
Async XLA Ops:
  0.6 0.7 %copy-start.1 = (f32[4]{0:T(128)S(1)}, f32[4]{0:T(128)}, u32[]{:S(2)}) copy-start(f32[4]{0:T(128)} %offsets_ref.1) | copy-start | bytes 52
  1.3 0.7 %copy-start.2 = (f32[16]{0:T(128)S(1)}, f32[16]{0:T(128)}, u32[]{:S(2)}) copy-start(f32[16]{0:T(128)} %velocities_ref.1) | copy-start | bytes 196
  2.1 0.7 %copy-start.3 = (s32[256,1]{0,1:T(1,128)S(1)}, s32[256,1]{0,1:T(1,128)}, u32[]{:S(2)}) copy-start(s32[256,1]{0,1:T(1,128)} %param.7) | copy-start | bytes 3076
  2.1 0.7 %copy-start.4 = (s32[256]{0:T(256)S(1)}, s32[256]{0:T(256)}, u32[]{:S(2)}) copy-start(s32[256]{0:T(256)} %param.8) | copy-start | bytes 3076
  2.1 0.7 %copy-start.5 = (s32[256]{0:T(256)S(1)}, s32[256]{0:T(256)}, u32[]{:S(2)}) copy-start(s32[256]{0:T(256)} %param.9) | copy-start | bytes 3076
  2.8 1.2 %copy-start = (bf16[256,2048]{1,0:T(8,128)(2,1)S(1)}, bf16[256,2048]{1,0:T(8,128)(2,1)}, u32[]{:S(2)}) copy-start(bf16[256,2048]{1,0:T(8,128)(2,1)} %traces_hbm.1) | copy-start | bytes 3145732

commit v6 on v5

--- a/solution.py
+++ b/solution.py
@@ -15,7 +15,7 @@
 VMEM_LIMIT = 24 << 20
 SUM_LAG = 2
 STACK_LAG = 4
-SIZES = (1, 2, 3, 3, 3, 2, 1, 1)
+SIZES = (1, 2, 2, 3, 3, 2, 2, 1)
 MESH = pl.DeviceIdType.MESH
 
 
@@ -447,7 +447,7 @@
             jax.ShapeDtypeStruct((mids, vels, samples), bf16),
             jax.ShapeDtypeStruct((mids, vels, samples), f32),
         ),
-        in_specs=[pl.BlockSpec(memory_space=pl.ANY), vmem, vmem, vmem, smem, smem, smem, vmem],
+        in_specs=[pl.BlockSpec(memory_space=pltpu.HBM), vmem, vmem, vmem, smem, smem, smem, vmem],
         out_specs=(vmem, vmem),
         scratch_shapes=[
             pltpu.VMEM((rows, samples), bf16),

time: 61.2 us -> 59.4 us (0.971)
  Pallas kernels: 55.1 us -> 53.4 us
    pallas_call x1, Pallas kernels: 55.1 us -> 53.4 us  [survey(): pl.pallas_call(functools.partial(kernel, dims), out_shape=(jax.ShapeDtype...]
where the time goes in v6:
time: 59.4 us; the launch traced here: 59.2 us
  Pallas kernels  53.4 us (90%)
  local copies, waits for them, and re-layouts  5.03 us (8%)
  between operations  0.7 us (1%)
    pallas_call x1, Pallas kernels, survey(): pl.pallas_call(functools.partial(kernel, dims), out_shape=(jax.ShapeDtype...  53.4 us
    unnamed x14, local copies, waits for them, and re-layouts  4.79 us

profile of v6, /device:TPU:1, one launch (start us, length us, event | category | flops | bytes accessed | tf_op | source)
XLA Modules:
  0.0 59.2 jit_solution(2855104716057406935)
XLA Ops:
  0.6 0.0 copy-start.1
  0.7 0.6 %copy-done.1 = f32[4]{0:T(128)S(1)} copy-done((f32[4]{0:T(128)S(1)}, f32[4]{0:T(128)}, u32[]{:S(2)}) %copy-start.1) | copy-done | bytes 40
  1.3 0.0 copy-start.2
  1.3 0.1 div.22
  1.4 0.6 copy-done.2
  1.9 0.1 div.23
  2.0 0.1 div.24
  2.1 0.0 copy-start.3
  2.1 0.0 copy-start.4
  2.1 0.0 copy-start.5
  2.2 0.1 minimum_convert_fusion.start_s.start_v
  2.2 0.6 copy-done.3
  2.8 0.0 copy-done.4
  2.8 0.0 copy-done.5
  2.8 0.0 copy-start
  2.8 1.2 %copy-done = bf16[256,2048]{1,0:T(8,128)(2,1)S(1)} copy-done((bf16[256,2048]{1,0:T(8,128)(2,1)S(1)}, bf16[256,2048]{1,0:T(8,128)(2,1)}, u32[]{:S(2)}) %copy-start) | copy-done | bytes 1048600
  4.1 53.4 %survey.1 = (bf16[8,16,2048]{2,1,0:T(8,128)(2,1)S(1)}, f32[8,16,2048]{2,1,0:T(8,128)S(1)}) custom-call(bf16[256,2048]{1,0:T(8,128)(2,1)S(1)} %copy-done, s32[1,256]{1,0:T(1,128)S(1)} %bitcast.5, s32[1,256]{1,0:T(1,128)S(1)} %bitcast.6, s32[1,256]{1,0:T(1,128)S(1)} %bitcast.7, f32[4]{0:T(128)S(1)} %copy-done.1, f32[16]{0:T(128)S(1)} %copy-done.2, ...), custom_call_target="tpu_custom_call" | custom-call | tf_op jit(solution)/shard_map/survey/pallas_call | solution.py:444
  57.5 0.8 %copy.11 = bf16[8,16,2048]{2,1,0:T(8,128)(2,1)} copy(bf16[8,16,2048]{2,1,0:T(8,128)(2,1)S(1)} %get-tuple-element.4) | data formatting | bytes 1048576
  58.2 1.0 %copy.12 = f32[8,16,2048]{2,1,0:T(8,128)} copy(f32[8,16,2048]{2,1,0:T(8,128)S(1)} %get-tuple-element.5) | data formatting | bytes 2097152
  (3 shorter events, 0.0 us)
Async XLA Ops:
  0.6 0.7 %copy-start.1 = (f32[4]{0:T(128)S(1)}, f32[4]{0:T(128)}, u32[]{:S(2)}) copy-start(f32[4]{0:T(128)} %offsets_ref.1) | copy-start | bytes 52
  1.3 0.7 %copy-start.2 = (f32[16]{0:T(128)S(1)}, f32[16]{0:T(128)}, u32[]{:S(2)}) copy-start(f32[16]{0:T(128)} %velocities_ref.1) | copy-start | bytes 196
  2.1 0.7 %copy-start.3 = (s32[256,1]{0,1:T(1,128)S(1)}, s32[256,1]{0,1:T(1,128)}, u32[]{:S(2)}) copy-start(s32[256,1]{0,1:T(1,128)} %param.7) | copy-start | bytes 3076
  2.1 0.7 %copy-start.4 = (s32[256]{0:T(256)S(1)}, s32[256]{0:T(256)}, u32[]{:S(2)}) copy-start(s32[256]{0:T(256)} %param.8) | copy-start | bytes 3076
  2.1 0.7 %copy-start.5 = (s32[256]{0:T(256)S(1)}, s32[256]{0:T(256)}, u32[]{:S(2)}) copy-start(s32[256]{0:T(256)} %param.9) | copy-start | bytes 3076
  2.8 1.2 %copy-start = (bf16[256,2048]{1,0:T(8,128)(2,1)S(1)}, bf16[256,2048]{1,0:T(8,128)(2,1)}, u32[]{:S(2)}) copy-start(bf16[256,2048]{1,0:T(8,128)(2,1)} %traces_hbm.1) | copy-start | bytes 3145732

commit v7 on v6

--- a/solution.py
+++ b/solution.py
@@ -11,7 +11,7 @@
 LANES = 128
 GROUP = 8
 HALF_WIN = 4
-AHEAD = 8
+AHEAD = 5
 VMEM_LIMIT = 24 << 20
 SUM_LAG = 2
 STACK_LAG = 4
@@ -478,7 +478,7 @@
         ],
         compiler_params=pltpu.CompilerParams(collective_id=0, has_side_effects=True, vmem_limit_bytes=VMEM_LIMIT),
         name="survey",
-    )(traces, owners, midpoint, offset_class, offsets, velocities, start, start)
+    )(pltpu.with_memory_space_constraint(traces, pltpu.HBM), owners, midpoint, offset_class, offsets, velocities, start, start)
 
 
 def per_device(traces, owners, midpoint, offset_class, offsets, velocities):

time: 59.4 us -> 58.3 us (0.981); the launches traced: 59.2 us -> 57.5 us
  local copies, waits for them, and re-layouts: 5.03 us -> 3.81 us
    unnamed x14 -> x12, local copies, waits for them, and re-layouts: 4.79 us -> 3.57 us
where the time goes in v7:
time: 58.3 us; the launch traced here: 57.5 us
  Pallas kernels  52.9 us (91%)
  local copies, waits for them, and re-layouts  3.81 us (7%)
  between operations  0.7 us (1%)
    pallas_call x1, Pallas kernels, survey(): pl.pallas_call(functools.partial(kernel, dims), out_shape=(jax.ShapeDtype...  52.9 us
    unnamed x12, local copies, waits for them, and re-layouts  3.57 us

profile of v7, /device:TPU:1, one launch (start us, length us, event | category | flops | bytes accessed | tf_op | source)
XLA Modules:
  0.0 57.5 jit_solution(6364250640460906065)
XLA Ops:
  0.6 0.0 copy-start
  0.7 0.6 %copy-done = f32[4]{0:T(128)S(1)} copy-done((f32[4]{0:T(128)S(1)}, f32[4]{0:T(128)}, u32[]{:S(2)}) %copy-start) | copy-done | bytes 40
  1.3 0.0 copy-start.1
  1.3 0.1 div.22
  1.4 0.6 copy-done.1
  1.9 0.1 div.23
  2.0 0.1 div.24
  2.1 0.0 copy-start.2
  2.1 0.0 copy-start.3
  2.1 0.0 copy-start.4
  2.2 0.1 minimum_convert_fusion.start_s.start_v
  2.2 0.6 copy-done.2
  2.8 0.0 copy-done.3
  2.8 0.0 copy-done.4
  2.8 52.9 %survey.1 = (bf16[8,16,2048]{2,1,0:T(8,128)(2,1)S(1)}, f32[8,16,2048]{2,1,0:T(8,128)S(1)}) custom-call(bf16[256,2048]{1,0:T(8,128)(2,1)} %traces_hbm.1, s32[1,256]{1,0:T(1,128)S(1)} %bitcast.5, s32[1,256]{1,0:T(1,128)S(1)} %bitcast.6, s32[1,256]{1,0:T(1,128)S(1)} %bitcast.7, f32[4]{0:T(128)S(1)} %copy-done, f32[16]{0:T(128)S(1)} %copy-done.1, ...), custom_call_target="tpu_custom_call" | custom-call | tf_op jit(solution)/shard_map/survey/pallas_call | solution.py:444
  55.7 0.8 %copy.11 = bf16[8,16,2048]{2,1,0:T(8,128)(2,1)} copy(bf16[8,16,2048]{2,1,0:T(8,128)(2,1)S(1)} %get-tuple-element.4) | data formatting | bytes 1048576
  56.5 1.0 %copy.12 = f32[8,16,2048]{2,1,0:T(8,128)} copy(f32[8,16,2048]{2,1,0:T(8,128)S(1)} %get-tuple-element.5) | data formatting | bytes 2097152
  (3 shorter events, 0.0 us)
Async XLA Ops:
  0.6 0.7 %copy-start = (f32[4]{0:T(128)S(1)}, f32[4]{0:T(128)}, u32[]{:S(2)}) copy-start(f32[4]{0:T(128)} %offsets_ref.1) | copy-start | bytes 52
  1.3 0.7 %copy-start.1 = (f32[16]{0:T(128)S(1)}, f32[16]{0:T(128)}, u32[]{:S(2)}) copy-start(f32[16]{0:T(128)} %velocities_ref.1) | copy-start | bytes 196
  2.1 0.7 %copy-start.2 = (s32[256,1]{0,1:T(1,128)S(1)}, s32[256,1]{0,1:T(1,128)}, u32[]{:S(2)}) copy-start(s32[256,1]{0,1:T(1,128)} %param.7) | copy-start | bytes 3076
  2.1 0.7 %copy-start.3 = (s32[256]{0:T(256)S(1)}, s32[256]{0:T(256)}, u32[]{:S(2)}) copy-start(s32[256]{0:T(256)} %param.8) | copy-start | bytes 3076
  2.1 0.7 %copy-start.4 = (s32[256]{0:T(256)S(1)}, s32[256]{0:T(256)}, u32[]{:S(2)}) copy-start(s32[256]{0:T(256)} %param.9) | copy-start | bytes 3076
